TPU v7x, 32 devices: a whole 2x2x4 slice. The times are simulated.
32 devices in a mesh: rows: 16 (over z, y, x), keys: 2 (over core).
Axes of the slice: x: 2, y: 2, z: 4, core: 2. Of those that a mesh axis runs over, the one named last changes fastest.
Arguments:
- tokens: bfloat16 [16, 1024, 768], P('rows', 'keys'), may hold values from -6 to 6
- seg_ids: int32 [16, 1024], P('rows'), may hold values from 0 to 7, as said below
- doc_starts: int32 [16, 1024], P('rows', 'keys'), may hold values from 0 to 1, as said below
- gain_in: float32 [768], replicated, may hold values from 0.1 to 1.9
- shift_in: float32 [768], replicated, may hold values from -3 to 3
- w_query: bfloat16 [768, 768], replicated, may hold values from -0.21875 to 0.21875
- w_key: bfloat16 [768, 768], replicated, may hold values from -0.21875 to 0.21875
- w_value: bfloat16 [768, 768], replicated, may hold values from -0.21875 to 0.21875
- w_out: bfloat16 [768, 768], replicated, may hold values from -0.625 to 0.625
- gain_mid: float32 [768], replicated, may hold values from 0.1 to 1.9
- shift_mid: float32 [768], replicated, may hold values from -3 to 3
- w_up: bfloat16 [768, 3072], replicated, may hold values from -0.21875 to 0.21875
- w_down: bfloat16 [3072, 768], replicated, may hold values from -0.109375 to 0.109375
- out_grad: bfloat16 [16, 1024, 768], P('rows', 'keys'), may hold values from -6 to 6
Outputs:
- output: bfloat16 [16, 1024, 768], P('rows', 'keys')
- input_grad: bfloat16 [16, 1024, 768], P('rows', 'keys')
- key_share: float32 [16, 1024], P('rows', 'keys')
- grad_gain_in: float32 [768], P('rows')
- grad_shift_in: float32 [768], P('rows')
- grad_w_query: float32 [768, 768], P('rows')
- grad_w_key: float32 [768, 768], P('rows')
- grad_w_value: float32 [768, 768], P('rows')
- grad_w_out: float32 [768, 768], P('rows')
- grad_gain_mid: float32 [768], P('rows')
- grad_shift_mid: float32 [768], P('rows')
- grad_w_up: float32 [768, 3072], P('rows')
- grad_w_down: float32 [3072, 768], P('rows')
Inputs may be any that keep to these rules, and one draw needn't show every extreme that they name: `seg_ids`: within each row the ids begin at 0 and rise by one at each document's first token; they never fall. Every row holds exactly 8 documents. `doc_starts`: 1 exactly at a row's first token and where seg_ids differs from the previous token's, else 0.
All inputs are finite; a program needn't handle non-finite values.
Results may differ from a plain program's by a relative error of at most 0.019.
Values may be sent and summed in bfloat16 or wider, within the bound.
A program may use at most 192 MiB of HBM per device.

v0:
```python
import functools

import jax
import jax.numpy as jnp
from jax import lax
from jax.experimental import pallas as pl
from jax.experimental.pallas import tpu as pltpu
from jax.sharding import PartitionSpec as P

HEAD = 64
PAIR = 2 * HEAD
TILE = 256
EPS = 1e-05
MASKED = 1e30
SELECT_SHIFT = 4.0
LOW = jnp.bfloat16
FULL = jnp.float32
MESH = pl.DeviceIdType.MESH
VMEM_LIMIT = 67_000_000


def contract(left, right, left_dim, right_dim):
    return lax.dot_general(
        left, right, (((left_dim,), (right_dim,)), ((), ())), preferred_element_type=FULL
    )


def layer_norm(field):
    center = field - jnp.mean(field, -1, keepdims=True)
    inverse = lax.rsqrt(jnp.mean(center * center, -1, keepdims=True) + EPS)
    return center * inverse, inverse


def remote(source, target, send, recv, device):
    return pltpu.make_async_remote_copy(
        src_ref=source,
        dst_ref=target,
        send_sem=send,
        recv_sem=recv,
        device_id=device,
        device_id_type=MESH,
    )


def lanes_below(shape, bound):
    return lax.broadcasted_iota(jnp.int32, shape, len(shape) - 1) < bound


def flat(ref):
    return ref[...].reshape(1, ref.shape[0])


def corner(step, tiles):
    t = sum((step >= n * (n + 1) // 2).astype(jnp.int32) for n in range(1, tiles))
    return t, step - t * (t + 1) // 2


def rows_of(start, size):
    return pl.ds(pl.multiple_of(start, size), size)


def attend_kernel(
    tokens,
    seg,
    gain,
    shift,
    w_query,
    w_key,
    w_value,
    low_in_out,
    query_out,
    key_out,
    value_out,
    prob_outs,
    slopes_out,
    heads_out,
    other_out,
    share_out,
    all_tokens,
    low_in,
    weights,
    queries,
    keys,
    values,
    lead_query,
    lead_key,
    probs,
    slopes,
    penalty,
    heads,
    seg_cols,
    free_cols,
    running,
    numerator,
    pairs_seen,
    far_send,
    far_recv,
    head_send,
    head_recv,
    weight_sems,
    out_sems,
    prob_sems,
):
    core = lax.axis_index("keys")
    row = lax.axis_index("rows")
    other = 1 - core
    partner = (row, other)
    half, width = tokens.shape
    length = 2 * half
    mine = width // 2
    pair_count = mine // PAIR
    tiles = length // TILE

    columns = pl.ds(pl.multiple_of(core * mine, 128), mine)
    loads = []
    for place, source in enumerate((w_query, w_key, w_value)):
        loads.append((source.at[:, columns], weights.at[:, pl.ds(place * mine, mine)]))
    for place, source in enumerate((w_query, w_key)):
        loads.append(
            (source.at[:, pl.ds(0, PAIR)], weights.at[:, pl.ds(3 * mine + place * PAIR, PAIR)])
        )
    own = rows_of(core * half, half)
    loads = [
        pltpu.make_async_copy(source, target, weight_sems.at[i])
        for i, (source, target) in enumerate(loads)
    ]
    own_load = pltpu.make_async_copy(tokens, all_tokens.at[own], weight_sems.at[5])
    own_load.start()
    for one in loads:
        one.start()

    barrier = pltpu.get_barrier_semaphore()
    pl.semaphore_signal(barrier, inc=1, device_id=partner, device_id_type=MESH)
    pl.semaphore_wait(barrier, 1)
    exchange = remote(tokens, all_tokens.at[own], far_send, far_recv, partner)
    exchange.start()

    seg_row = seg[...]
    seg_wide = jnp.broadcast_to(seg_row.astype(FULL), (128, length))
    spot = lax.broadcasted_iota(jnp.int32, (128, length), 1)
    before = pltpu.roll(seg_wide, 1, 1)
    free_wide = jnp.where((spot > 0) & (before == seg_wide), 1.0, 0.0)
    seg_cols[...] = seg_wide.T
    free_cols[...] = free_wide.T
    own_load.wait()

    keep = lanes_below((TILE, PAIR), HEAD)

    @pl.loop(0, tiles)
    def _(i):
        @pl.when(i == half // TILE)
        def _():
            exchange.wait_recv()

        here = rows_of(lax.rem(core * (half // TILE) + i, tiles) * TILE, TILE)
        unit, _ = layer_norm(all_tokens[here, :].astype(FULL))
        low_in[here, :] = (unit * flat(gain) + flat(shift)).astype(LOW)

        @pl.when(i == 0)
        def _():
            for one in loads:
                one.wait()

        result = contract(low_in[here, :], weights[...], 1, 0).astype(LOW)
        for p in range(pair_count):
            queries[p, here, :] = result[:, p * PAIR : (p + 1) * PAIR] * LOW(0.125)
            keys[p, here, :] = result[:, mine + p * PAIR : mine + (p + 1) * PAIR]
            values[p, here, :] = result[:, 2 * mine + p * PAIR : 2 * mine + (p + 1) * PAIR]
        first = result[:, 3 * mine : 3 * mine + PAIR]
        lead_query[here, :] = jnp.where(keep, first, LOW(0.0)) * LOW(0.125)
        lead_key[here, :] = result[:, 3 * mine + PAIR :]

    puts = [
        pltpu.make_async_copy(low_in, low_in_out, out_sems.at[0]),
        pltpu.make_async_copy(queries, query_out, out_sems.at[1]),
        pltpu.make_async_copy(keys, key_out, out_sems.at[2]),
        pltpu.make_async_copy(values, value_out, out_sems.at[3]),
    ]
    for one in puts:
        one.start()

    spots = (
        lax.broadcasted_iota(jnp.int32, (TILE, 2 * TILE), 0),
        lax.broadcasted_iota(jnp.int32, (TILE, 2 * TILE), 1),
    )
    pairs = (
        lax.broadcasted_iota(jnp.int32, (2 * TILE, 2 * TILE), 0),
        lax.broadcasted_iota(jnp.int32, (2 * TILE, 2 * TILE), 1),
    )
    earlier = jnp.where(pairs[0] < pairs[1], 1.0, 0.0).astype(LOW)
    running[...] = jnp.zeros_like(running)
    numerator[...] = jnp.zeros_like(numerator)
    pairs_seen[...] = jnp.zeros_like(pairs_seen)

    @pl.loop(0, (tiles // 2) * (tiles // 2 + 1))
    def _(step):
        wide = sum((step >= n * (n + 1)).astype(jnp.int32) for n in range(1, tiles // 2))
        k = step - wide * (wide + 1)
        rows, span = rows_of(k * TILE, TILE), rows_of(wide * 2 * TILE, 2 * TILE)
        scores = contract(lead_key[rows, :], lead_query[span, :], 1, 1)
        repeat = 2 * TILE // 128
        same = jnp.concatenate([seg_cols[rows, :]] * repeat, 1) == seg[:, span].astype(FULL)
        ahead = spots[1] - spots[0] + (2 * wide - k) * TILE
        later = same & (ahead > 0)
        allowed = same & (ahead >= 0)
        select = jnp.where(later, jnp.concatenate([free_cols[rows, :]] * repeat, 1), 0.0)
        level = scores - SELECT_SHIFT
        chosen = select * (jnp.maximum(level, 0.0) + jnp.log(1.0 + jnp.exp(-jnp.abs(level))))
        slope = (select * (0.5 + 0.5 * jnp.tanh(0.5 * level))).astype(LOW)

        @pl.when(k <= 2 * wide)
        def _():
            slopes[wide * (2 * wide + 1) + k] = slope[:, :TILE]

        slopes[(2 * wide + 1) * (wide + 1) + k] = slope[:, TILE:]
        high = chosen.astype(LOW)
        rest = (chosen - high.astype(FULL)).astype(LOW)
        total = (
            running[rows, :] + contract(high, earlier, 1, 0) + contract(rest, earlier, 1, 0)
        )
        penalty[rows, span] = jnp.where(allowed, total, MASKED)
        running[rows, :] += jnp.sum(chosen, -1, keepdims=True)
        share = jnp.where(later, 0.5 + 0.5 * jnp.tanh(0.5 * total - 1.0), 0.0)
        numerator[rows, :] += jnp.sum(share, -1, keepdims=True)
        pairs_seen[rows, :] += jnp.sum(jnp.where(later, 1.0, 0.0), -1, keepdims=True)

    slope_put = pltpu.make_async_copy(slopes, slopes_out, out_sems.at[4])
    slope_put.start()

    shares = numerator[own, :] / jnp.maximum(pairs_seen[own, :], 1.0)
    share_out[...] = jnp.broadcast_to(shares, (half, 128)).T[0:8, :]

    def put_probs(p, t):
        return pltpu.make_async_copy(
            probs[t].at[p], prob_outs[t].at[p], prob_sems.at[p, t]
        )

    def send_heads(p):
        return remote(
            heads.at[p, rows_of(other * half, half)],
            other_out.at[p],
            head_send.at[p],
            head_recv.at[p],
            partner,
        )

    @pl.loop(0, pair_count)
    def _(p):
        for t in range(tiles):
            count = (t + 1) * TILE
            span = pl.ds(t * TILE, TILE)
            query = queries[p, span, :]
            outs = []
            for h in range(2):
                masked = jnp.where(keep == (h == 0), query, LOW(0.0))
                logits = (
                    contract(keys[p, pl.ds(0, count), :], masked, 1, 1)
                    - penalty[pl.ds(0, count), span]
                )
                scaled = jnp.exp(logits - jnp.max(logits, 0, keepdims=True))
                prob = (scaled * (1.0 / jnp.sum(scaled, 0, keepdims=True))).astype(LOW)
                probs[t][p, :, pl.ds(h * TILE, TILE)] = prob
                out = contract(values[p, pl.ds(0, count), :], prob, 0, 0)
                outs.append(out[h * HEAD : (h + 1) * HEAD, :])
            heads[p, span, :] = jnp.concatenate(outs, 0).T.astype(LOW)
            put_probs(p, t).start()
        send_heads(p).start()

    last = pltpu.make_async_copy(heads, heads_out, out_sems.at[5])
    last.start()
    for p in range(pair_count):
        send_heads(p).wait()
        for t in range(tiles):
            put_probs(p, t).wait()
    for one in puts + [slope_put, last]:
        one.wait()
    exchange.wait_send()


def attend(tokens, seg, gain, shift, w_query, w_key, w_value):
    half, width = tokens.shape
    length, mine = 2 * half, width // 2
    pairs, tiles = mine // PAIR, 2 * half // TILE
    spans = [(t + 1) * TILE for t in range(tiles)]
    corners = tiles * (tiles + 1) // 2
    outs = [
        jax.ShapeDtypeStruct((length, width), LOW),
        jax.ShapeDtypeStruct((pairs, length, PAIR), LOW),
        jax.ShapeDtypeStruct((pairs, length, PAIR), LOW),
        jax.ShapeDtypeStruct((pairs, length, PAIR), LOW),
        [jax.ShapeDtypeStruct((pairs, span, 2 * TILE), LOW) for span in spans],
        jax.ShapeDtypeStruct((corners, TILE, TILE), LOW),
        jax.ShapeDtypeStruct((pairs, length, PAIR), LOW),
        jax.ShapeDtypeStruct((pairs, half, PAIR), LOW),
        jax.ShapeDtypeStruct((8, half), FULL),
    ]
    anywhere = pl.BlockSpec(memory_space=pl.ANY)
    local = pl.BlockSpec(memory_space=pltpu.VMEM)
    out_specs = [anywhere] * 4 + [[anywhere] * tiles, anywhere, anywhere, anywhere, local]
    scratch = [
        pltpu.VMEM((length, width), LOW),
        pltpu.VMEM((length, width), LOW),
        pltpu.VMEM((width, 3 * mine + 2 * PAIR), LOW),
        pltpu.VMEM((pairs, length, PAIR), LOW),
        pltpu.VMEM((pairs, length, PAIR), LOW),
        pltpu.VMEM((pairs, length, PAIR), LOW),
        pltpu.VMEM((length, PAIR), LOW),
        pltpu.VMEM((length, PAIR), LOW),
        [pltpu.VMEM((pairs, span, 2 * TILE), LOW) for span in spans],
        pltpu.VMEM((corners, TILE, TILE), LOW),
        pltpu.VMEM((length, length), FULL),
        pltpu.VMEM((pairs, length, PAIR), LOW),
        pltpu.VMEM((length, 128), FULL),
        pltpu.VMEM((length, 128), FULL),
        pltpu.VMEM((length, 1), FULL),
        pltpu.VMEM((length, 1), FULL),
        pltpu.VMEM((length, 1), FULL),
        pltpu.SemaphoreType.DMA,
        pltpu.SemaphoreType.DMA,
        pltpu.SemaphoreType.DMA((pairs,)),
        pltpu.SemaphoreType.DMA((pairs,)),
        pltpu.SemaphoreType.DMA((6,)),
        pltpu.SemaphoreType.DMA((6,)),
        pltpu.SemaphoreType.DMA((pairs, tiles)),
    ]
    return pl.pallas_call(
        attend_kernel,
        out_shape=outs,
        in_specs=[anywhere] + [local] * 3 + [anywhere] * 3,
        out_specs=out_specs,
        scratch_shapes=scratch,
        compiler_params=pltpu.CompilerParams(
            collective_id=1, has_side_effects=True, vmem_limit_bytes=VMEM_LIMIT
        ),
        name="attend",
    )(tokens, seg, gain, shift, w_query, w_key, w_value)

def gelu_parts(field):
    scale = 0.7978845608028654
    square = field * field
    inner = jnp.tanh(scale * field * (1.0 + 0.044715 * square))
    half_sum = 0.5 * (1.0 + inner)
    slope = half_sum + 0.5 * field * (1.0 - inner * inner) * (
        scale * (1.0 + 3.0 * 0.044715 * square)
    )
    return field * half_sum, slope


GRID = (4, 2, 2)
COUNT = GRID[0] * GRID[1] * GRID[2]
KINDS = ("down", "up", "out", "attn", "early", "lead", "vec")
FAN = {"down": 1, "up": 2, "out": 1, "attn": 2, "early": 1, "lead": 1, "vec": 1}


def block_shapes(width, hidden):
    mine = width // 2
    tall = width // COUNT
    return {
        "down": ((hidden // COUNT, mine), LOW),
        "up": ((tall, mine * 2), LOW),
        "out": ((tall, mine), LOW),
        "attn": ((tall, mine), LOW),
        "early": ((tall, 2 * PAIR), LOW),
        "lead": ((tall, PAIR), LOW),
        "vec": ((8, 128), FULL),
    }


def finish_kernel(fused, *refs):
    refs = list(refs)

    def take(count):
        taken = refs[:count]
        del refs[:count]
        return taken if count > 1 else taken[0]

    tokens, cotangent, gain_in, gain_mid, shift_mid = take(5)
    low_in_hbm, query_hbm, key_hbm, value_hbm = take(4)
    prob_hbm, slope_hbm = take(4), take(1)
    heads_hbm, other_hbm = take(2)
    w_query, w_key, w_value, w_out, w_up, w_down = take(6)
    output, input_grad = take(2)
    results = dict(zip(KINDS, take(len(KINDS))))
    (
        grads_all,
        weight_out,
        heads,
        heads_far,
        resid,
        low_mid,
        grad_resid,
        low_resid,
        grad_heads,
        low_in,
        queries,
        keys,
        values,
    ) = take(13)
    probs = take(4)
    share_send, share_recv = take(2)
    stage, stage_far, catch_mid, catch_out = take(4)
    weight_down, hidden_low = take(2)
    stage_down, stage_out = take(2)
    vec_sums = take(1)
    parts = dict(zip(KINDS, take(len(KINDS))))
    if fused:
        got1 = dict(zip(KINDS, take(len(KINDS))))
        got2 = dict(zip(KINDS, take(len(KINDS))))
        got3 = dict(zip(KINDS, take(len(KINDS))))
        pair = dict(zip(KINDS, take(len(KINDS))))
        sems = {
            name: take(2) for name in ("down1", "down2", "down3", "down4")
        }
        for kind in KINDS[1:]:
            for stage_name in "1234":
                sems[kind + stage_name] = take(2)
    (load_sems, g_sems, mid_sems, dz_sems, a_sems, b_sems, c_sems, pd_sems, po_sems, df_sems, prob_sems) = take(11)

    long, wide, deep = GRID
    core = lax.axis_index("keys")
    row = lax.axis_index("rows")
    other = 1 - core
    partner = (row, other)
    half, width = tokens.shape
    length, mine = 2 * half, width // 2
    pair_count = mine // PAIR
    tiles = length // TILE
    hidden = w_down.shape[0]
    block = hidden // 4
    own_start, far_start = core * half, other * half

    if fused:
        slow, mid, fast = row // (wide * deep), (row // deep) % wide, row % deep
    else:
        slow, mid, fast = 0, 0, 0

    def spot_of(rank, whose):
        z, y, x = rank // (wide * deep), (rank // deep) % wide, rank % deep
        if not fused:
            return z, y, x
        return z, x + whose * (y - x), y + whose * (x - y)

    first, second = fast + core * (mid - fast), mid + core * (fast - mid)
    near, next_ = 1 - first, 1 - second

    def rank_of(z, a, b):
        y, x = b + core * (a - b), a + core * (b - a)
        return (z * wide + y) * deep + x

    near_device = (rank_of(slow, near, second), core)
    next_device = (rank_of(slow, first, next_), core)
    far_places = [lax.rem(slow + step, long) for step in range(1, long)]

    def add_into(target, index, terms):
        total = target[index].astype(FULL)
        for term in terms:
            total = total + term.astype(FULL)
        target[index] = total.astype(target.dtype)

    class Job:
        def __init__(self, kind, k):
            self.kind, self.k = kind, k

        def first_copy(self):
            kind, k = self.kind, self.k
            part, got = parts[kind].at[k], got1[kind].at[k]
            send, recv = sems[kind + "1"]
            return remote(part.at[:, near], got, send.at[k], recv.at[k], near_device)

        def second_copy(self):
            kind, k = self.kind, self.k
            part, got = parts[kind].at[k], got2[kind].at[k]
            send, recv = sems[kind + "2"]
            return remote(part.at[:, first, next_], got, send.at[k], recv.at[k], next_device)

        def third_copies(self):
            kind, k = self.kind, self.k
            send, recv = sems[kind + "3"]
            return [
                remote(
                    parts[kind].at[k, z, first, second],
                    got3[kind].at[k, step],
                    send.at[k, step],
                    recv.at[k, step],
                    (rank_of(z, first, second), core),
                )
                for step, z in enumerate(far_places)
            ]

        def last_copy(self):
            kind, k = self.kind, self.k
            send, recv = sems[kind + "4"]
            return remote(
                parts[kind].at[k, slow, first, second],
                pair[kind].at[k],
                send.at[k],
                recv.at[k],
                partner,
            )

        def start(self):
            self.first_copy().start()

        def turn(self):
            self.first_copy().wait_recv()
            kind, k = self.kind, self.k

            @pl.loop(0, long * deep)
            def _(step):
                z, b = step // deep, lax.rem(step, deep)
                add_into(parts[kind], (k, z, first, b), [got1[kind][k, z, b]])

            self.second_copy().start()

        def gather(self):
            self.second_copy().wait_recv()
            kind, k = self.kind, self.k

            @pl.loop(0, long)
            def _(z):
                add_into(parts[kind], (k, z, first, second), [got2[kind][k, z]])

            for one in self.third_copies():
                one.start()

        def close(self):
            for one in self.third_copies():
                one.wait_recv()
            kind, k = self.kind, self.k
            add_into(
                parts[kind],
                (k, slow, first, second),
                [got3[kind][k, step] for step in range(long - 1)],
            )
            self.last_copy().start()

        def store(self):
            self.last_copy().wait_recv()
            kind, k = self.kind, self.k
            results[kind][k, core] = parts[kind][k, slow, first, second]
            results[kind][k, other] = pair[kind][k]

        def drain(self):
            self.first_copy().wait_send()
            self.second_copy().wait_send()
            for one in self.third_copies():
                one.wait_send()
            self.last_copy().wait_send()

    class Down(Job):
        def near_copy(self, z):
            send, recv = sems["down1"]
            return remote(
                parts["down"].at[0, z, near],
                got1["down"].at[0, z],
                send.at[z],
                recv.at[z],
                near_device,
            )

        def slow_copy(self, step):
            z = lax.rem(slow + step, long)
            send, recv = sems["down2"]
            return remote(
                parts["down"].at[0, z, first],
                got2["down"].at[0, step - 1],
                send.at[step - 1],
                recv.at[step - 1],
                (rank_of(z, first, second), core),
            )

        def next_copy(self):
            send, recv = sems["down3"]
            return remote(
                parts["down"].at[0, slow, first, next_],
                got3["down"].at[0],
                send.at[0],
                recv.at[0],
                next_device,
            )

        def start_at(self, z):
            self.near_copy(z).start()

        def turn_at(self, z):
            self.near_copy(z).wait_recv()

            @pl.loop(0, deep)
            def _(b):
                add_into(parts["down"], (0, z, first, b), [got1["down"][0, z, b]])

            step = lax.rem(z - slow + long, long)

            @pl.when(step > 0)
            def _():
                self.slow_copy(step).start()

        def cross(self):
            for step in range(1, long):
                self.slow_copy(step).wait_recv()

            @pl.loop(0, deep)
            def _(b):
                add_into(
                    parts["down"],
                    (0, slow, first, b),
                    [got2["down"][0, step, b] for step in range(long - 1)],
                )

            self.next_copy().start()

        def close(self):
            self.next_copy().wait_recv()
            add_into(parts["down"], (0, slow, first, second), [got3["down"][0]])
            self.last_copy().start()

        def drain(self):
            for z in range(long):
                self.near_copy(z).wait_send()
            for step in range(1, long):
                self.slow_copy(step).wait_send()
            self.next_copy().wait_send()
            self.last_copy().wait_send()

    class Vectors(Job):
        def first_copies(self):
            send, recv = sems["vec1"]
            places = ((near, second), (first, next_), (near, next_))
            return [
                remote(
                    parts["vec"].at[0, :, a, b],
                    got1["vec"].at[0, i],
                    send.at[i],
                    recv.at[i],
                    (rank_of(slow, a, b), core),
                )
                for i, (a, b) in enumerate(places)
            ]

        def start(self):
            for one in self.first_copies():
                one.start()

        def gather(self):
            for one in self.first_copies():
                one.wait_recv()

            @pl.loop(0, long)
            def _(z):
                add_into(
                    parts["vec"], (0, z, first, second), [got1["vec"][0, i, z] for i in range(3)]
                )

            for one in self.third_copies():
                one.start()

        def drain(self):
            for one in self.first_copies() + self.third_copies():
                one.wait_send()
            self.last_copy().wait_send()

    def steps(*names):
        if fused:
            for name in names:
                job, step = name.split()
                getattr(jobs[job], step)()

    def steps_when(condition, *names):
        if fused:
            pl.when(condition)(lambda: steps(*names))

    down = Down("down", 0)
    jobs = {"down": down, "vec": Vectors("vec", 0)}
    jobs |= {kind: Job(kind, 0) for kind in ("out", "early", "lead")}
    jobs |= {f"up{k}": Job("up", k) for k in range(2)}
    jobs |= {f"attn{k + 1}": Job("attn", k) for k in range(pair_count - 1)}

    def local(source, target, index):
        return pltpu.make_async_copy(source, target, load_sems.at[index])

    own = rows_of(own_start, half)
    in_put = local(low_mid.at[pl.ds(0, half)], input_grad, 0)
    out_put = local(low_mid.at[pl.ds(half, half)], output, 1)
    g_load = local(cotangent, grads_all.at[own], 0)
    out_loads = [
        local(w_out.at[rows_of(core * mine, mine)], weight_out.at[pl.ds(0, mine)], 1),
        local(w_out.at[rows_of(other * mine, mine)], weight_out.at[pl.ds(mine, mine)], 2),
        local(heads_hbm, heads, 3),
        local(other_hbm, heads_far, 4),
    ]
    late_loads = [
        local(low_in_hbm, low_in, 5),
        local(query_hbm, queries, 6),
        local(key_hbm, keys, 7),
        local(value_hbm, values, 8),
    ]
    for one in out_loads + [g_load]:
        one.start()

    peers = [partner]
    if fused:
        peers += [near_device, next_device, (rank_of(slow, near, next_), core)]
        peers += [(rank_of(z, first, second), core) for z in far_places]
    barrier = pltpu.get_barrier_semaphore()
    for peer in peers:
        pl.semaphore_signal(barrier, inc=1, device_id=peer, device_id_type=MESH)

    def own_rows(i):
        return rows_of(own_start + i * TILE, TILE)

    def far_rows(i):
        return rows_of(far_start + i * TILE, TILE)

    def tile_rows(i):
        return rows_of(i * TILE, TILE)

    def to_partner(source, target, pair_sems):
        def one(i):
            return remote(
                source(i), target(i), pair_sems.at[0, i], pair_sems.at[1, i], partner
            )

        return one

    g_far = remote(cotangent, grads_all.at[own], g_sems.at[0], g_sems.at[1], partner)
    mid_far = to_partner(
        lambda i: low_mid.at[own_rows(i)], lambda i: low_mid.at[own_rows(i)], mid_sems
    )
    dz_far = to_partner(
        lambda i: low_resid.at[own_rows(i)], lambda i: low_resid.at[own_rows(i)], dz_sems
    )
    mid_back = to_partner(
        lambda i: stage.at[tile_rows(i)], lambda i: catch_mid.at[tile_rows(i)], a_sems
    )
    in_back = to_partner(
        lambda i: stage.at[tile_rows(i)], lambda i: catch_mid.at[tile_rows(i)], b_sems
    )
    out_back = to_partner(
        lambda i: stage_far.at[tile_rows(i)], lambda i: catch_out.at[tile_rows(i)], c_sems
    )

    def feed_forward(weight_up, grad_up):
        up_loads = [
            local(
                w_up.at[:, pl.ds(pl.multiple_of((core * 2 + b) * block, 128), block)],
                weight_up.at[b],
                9 + b,
            )
            for b in range(2)
        ]
        down_loads = [
            local(w_down.at[rows_of((core * 2 + b) * block, block)], weight_down.at[b], 11 + b)
            for b in range(2)
        ]
        for b in range(2):
            up_loads[b].start()
            down_loads[b].start()
        for one in out_loads:
            one.wait()

        @pl.loop(0, 2)
        def _(i):
            here, place = tile_rows(i), own_rows(i)
            joined = jnp.concatenate(
                [heads[p, place, :] for p in range(pair_count)]
                + [heads_far[p, here, :] for p in range(pair_count)],
                1,
            )
            field = tokens[here, :].astype(FULL) + contract(joined, weight_out[...], 1, 0)
            resid[here, :] = field
            unit, _ = layer_norm(field)
            low_mid[place, :] = (unit * flat(gain_mid) + flat(shift_mid)).astype(LOW)

        pl.semaphore_wait(barrier, len(peers))
        g_far.start()
        for i in range(2):
            mid_far(i).start()

        for one in up_loads + down_loads + [g_load]:
            one.wait()
        for one in late_loads:
            one.start()

        @pl.loop(0, 2)
        def _(b):
            @pl.loop(0, tiles)
            def _(i):
                @pl.when((b == 0) & (i == 2))
                def _():
                    for j in range(2):
                        mid_far(j).wait_recv()

                here = rows_of(lax.rem(core * 2 + i, tiles) * TILE, TILE)
                value, slope = gelu_parts(contract(low_mid[here, :], weight_up[b], 1, 0))
                hidden_low[b, here, :] = value.astype(LOW)
                grad_up[b, here, :] = slope.astype(LOW)
                if fused:

                    @pl.when((b == 1) & (i == 0))
                    def _():
                        down.turn_at(core * 2)

                    @pl.when((b == 1) & (i == 2))
                    def _():
                        down.turn_at(other * 2)

            @pl.when(b == 0)
            def _():
                g_far.wait_recv()

            tall = hidden // COUNT
            per = mine // tall
            @pl.loop(0, 2)
            def _(m):
                place = pl.ds(pl.multiple_of(m * mine, 128), mine)
                grad = contract(hidden_low[b, :, place], grads_all[...], 0, 0).astype(LOW)
                kept = jnp.where(core == 0, grad[:, :mine], grad[:, mine:])
                given = jnp.where(core == 0, grad[:, mine:], grad[:, :mine])
                for i in range(per):
                    rank = (core * 2 + b) * (COUNT // 4) + m * per + i
                    z, a, s = spot_of(rank, core)
                    parts["down"][0, z, a, s] = kept[i * tall : (i + 1) * tall]
                    _, a, s = spot_of(rank, other)
                    stage_down[b, a, s] = given[i * tall : (i + 1) * tall]
            give_down(b).start()
            if fused:
                down.start_at(core * 2 + b)

            @pl.loop(0, tiles)
            def _(i):
                here = rows_of(i * TILE, TILE)
                back = contract(grads_all[here, :], weight_down[b], 1, 1)
                grad_up[b, here, :] = (back * grad_up[b, here, :].astype(FULL)).astype(LOW)

                @pl.when(i == 1)
                def _():
                    give_down(b).wait_recv()
                    if fused:
                        down.start_at(other * 2 + b)

                steps_when((b == 1) & (i == 2), "up0 turn")

            @pl.loop(0, 2)
            def _(m):
                tall = width // COUNT
                per = mine // tall
                place = pl.ds(pl.multiple_of(m * mine, 128), mine)
                grad = contract(low_mid[:, place], grad_up[b], 0, 0).astype(LOW)
                for i in range(per):
                    z, a, s = spot_of(m * per + i, core)
                    parts["up"][b, z, a, s] = grad[i * tall : (i + 1) * tall]

            if fused:
                Job("up", b).start()

        def mid_part(here):
            return contract(grad_up[0, here, :], weight_up[0], 1, 1) + contract(
                grad_up[1, here, :], weight_up[1], 1, 1
            )

        @pl.loop(0, tiles)
        def _(i):
            part = mid_part(rows_of(lax.rem(other * 2 + i, tiles) * TILE, TILE))

            @pl.when(i < 2)
            def _():
                stage[tile_rows(i), :] = part.astype(LOW)
                mid_back(i).start()

            @pl.when(i >= 2)
            def _():
                grad_resid[tile_rows(i - 2), :] = part

            if fused:

                @pl.when(i == 1)
                def _():
                    down.turn_at(core * 2 + 1)

        if fused:
            down.turn_at(other * 2 + 1)
        steps("up0 gather")

        @pl.loop(0, 2)
        def _(i):
            here = tile_rows(i)
            mid_back(i).wait_recv()
            grad = grad_resid[here, :] + catch_mid[here, :].astype(FULL)
            unit, inverse = layer_norm(resid[here, :])
            vec_sums[2:3, :] += jnp.sum(grad * unit, 0, keepdims=True)
            vec_sums[3:4, :] += jnp.sum(grad, 0, keepdims=True)
            scaled = grad * flat(gain_mid)
            total = grads_all[own_rows(i), :].astype(FULL) + inverse * (
                scaled
                - jnp.mean(scaled, -1, keepdims=True)
                - unit * jnp.mean(scaled * unit, -1, keepdims=True)
            )
            grad_resid[here, :] = total
            low_resid[own_rows(i), :] = total.astype(LOW)
            dz_far(i).start()

        for i in range(2):
            mid_back(i).wait_send()

    def give_down(b):
        return remote(
            stage_down.at[b],
            parts["down"].at[0, core * 2 + b],
            pd_sems.at[0, b],
            pd_sems.at[1, b],
            partner,
        )

    give_out = remote(
        stage_out,
        parts["out"].at[0, pl.ds(core * 2, 2)],
        po_sems.at[0],
        po_sems.at[1],
        partner,
    )

    vec_sums[...] = jnp.zeros_like(vec_sums)
    pl.run_scoped(
        feed_forward,
        pltpu.VMEM((2, width, block), LOW),
        pltpu.VMEM((2, length, block), LOW),
    )

    def prob_load(p, t):
        return pltpu.make_async_copy(prob_hbm[t].at[p], probs[t], prob_sems.at[t])

    def attention(slopes, fades, key_sum, value_sum, carry, grad_qkv, weight_in):
        for t in range(tiles):
            prob_load(pair_count - 1, t).start()
        slope_load = local(slope_hbm, slopes, 13)
        weight_loads = []
        for place, source in enumerate((w_query, w_key, w_value)):
            for p in range(pair_count):
                weight_loads.append(
                    local(
                        source.at[:, pl.ds(pl.multiple_of(core * mine + p * PAIR, 128), PAIR)],
                        weight_in.at[:, pl.ds(p * mine + place * PAIR, PAIR)],
                        17 + place * pair_count + p,
                    )
                )
        for one in [slope_load] + weight_loads:
            one.start()

        def head_grads(here):
            result = contract(low_resid[here, :], weight_out[pl.ds(0, mine), :], 1, 1).astype(LOW)
            for p in range(pair_count):
                grad_heads[p, here, :] = result[:, p * PAIR : (p + 1) * PAIR]

        @pl.loop(0, tiles)
        def _(i):
            @pl.when(i > 1)
            def _():
                dz_far(i - 2).wait_recv()

            head_grads(rows_of(lax.rem(core * 2 + i, tiles) * TILE, TILE))

        joined = jnp.concatenate([heads[p] for p in range(pair_count)], 1)
        grad = contract(joined, low_resid[...], 0, 0).astype(LOW)
        kept = jnp.where(core == 0, grad[:, :mine], grad[:, mine:])
        given = jnp.where(core == 0, grad[:, mine:], grad[:, :mine])
        tall = width // COUNT
        for i in range(mine // tall):
            rank = core * (COUNT // 2) + i
            z, a, s = spot_of(rank, core)
            parts["out"][0, z, a, s] = kept[i * tall : (i + 1) * tall]
            _, a, s = spot_of(rank, other)
            stage_out[i // (wide * deep), a, s] = given[i * tall : (i + 1) * tall]
        give_out.start()
        for one in late_loads:
            one.wait()
        give_out.wait_recv()
        steps("out start", "up1 turn")

        keep = lanes_below((TILE, PAIR), HEAD)
        spots = (
            lax.broadcasted_iota(jnp.int32, (TILE, TILE), 0),
            lax.broadcasted_iota(jnp.int32, (TILE, TILE), 1),
        )
        after = jnp.where(spots[0] > spots[1], 1.0, 0.0).astype(LOW)

        def fade_send(t):
            part = pl.ds(t * (t + 1) // 2, t + 1)
            return remote(
                share_send.at[part],
                share_recv.at[part],
                df_sems.at[0, t],
                df_sems.at[1, t],
                partner,
            )

        def pair_step(step, p):
            for t in reversed(range(tiles)):
                count = (t + 1) * TILE
                span, rows = pl.ds(t * TILE, TILE), pl.ds(0, count)
                prob_load(p, t).wait()
                grad_tile = grad_heads[p, span, :]
                product = (grad_tile.astype(FULL) * heads[p, span, :].astype(FULL)).T
                query = queries[p, span, :]
                grads, masked_q, masked_g = [], [], []
                fade = None
                for h in range(2):
                    mask = keep == (h == 0)
                    masked_g.append(jnp.where(mask, grad_tile, LOW(0.0)))
                    masked_q.append(jnp.where(mask, query, LOW(0.0)))
                    delta = jnp.sum(product[h * HEAD : (h + 1) * HEAD, :], 0, keepdims=True)
                    change = probs[t][:, pl.ds(h * TILE, TILE)].astype(FULL) * (
                        contract(values[p, rows, :], masked_g[h], 1, 1) - delta
                    )
                    fade = change if fade is None else fade + change
                    grads.append(change.astype(LOW))

                @pl.when(step == 0)
                def _():
                    fades[rows, span] = fade

                @pl.when(step > 0)
                def _():
                    fades[rows, span] += fade

                both = jnp.concatenate(grads, 1)
                key_part = contract(both, jnp.concatenate(masked_q, 0), 1, 0)
                value_part = contract(probs[t][...], jnp.concatenate(masked_g, 0), 1, 0)
                if t == tiles - 1:
                    key_sum[...] = key_part
                    value_sum[...] = value_part
                else:
                    key_sum[rows, :] += key_part
                    value_sum[rows, :] += value_part
                query_part = contract(keys[p, rows, :], both, 0, 0)
                query_part = jnp.concatenate(
                    [query_part[:HEAD, :TILE], query_part[HEAD:, TILE:]], 0
                )
                grad_qkv[p, span, pl.ds(0, PAIR)] = (query_part.T * 0.125).astype(LOW)

                @pl.when(step < pair_count - 1)
                def _():
                    prob_load(p - 1, t).start()

                @pl.when((step == pair_count - 1) & (core == 1))
                def _():
                    share_send[pl.ds(t * (t + 1) // 2, t + 1)] = (
                        fades[rows, span].astype(LOW).reshape(t + 1, TILE, TILE)
                    )
                    fade_send(t).start()

        def lead_head():
            @pl.when(core == 0)
            def _():
                carry[...] = jnp.zeros_like(carry)
                for t in reversed(range(tiles)):
                    count = (t + 1) * TILE
                    span, rows = pl.ds(t * TILE, TILE), pl.ds(0, count)
                    part = pl.ds(t * (t + 1) // 2, t + 1)
                    fade_send(t).wait_recv()
                    total = fades[rows, span] + share_recv[part].astype(FULL).reshape(count, TILE)
                    later = contract(total.astype(LOW), after, 1, 0) + carry[rows, :]
                    if t:
                        carry[rows, :] += jnp.sum(total, -1, keepdims=True)
                    slope = slopes[part].astype(FULL).reshape(count, TILE)
                    extra = (-later * slope).astype(LOW)
                    query = jnp.where(keep, queries[0, span, :], LOW(0.0))
                    key_sum[rows, :] += contract(extra, query, 1, 0)
                    whole = contract(keys[0, rows, :], extra, 0, 0).T * 0.125
                    grad_qkv[0, span, pl.ds(0, PAIR)] = (
                        grad_qkv[0, span, pl.ds(0, PAIR)].astype(FULL)
                        + jnp.where(keep, whole, 0.0)
                    ).astype(LOW)

            @pl.when(core == 1)
            def _():
                for t in range(tiles):
                    fade_send(t).wait_send()

        def weights_into(kind, k, right):
            @pl.loop(0, 2)
            def _(m):
                place = pl.ds(pl.multiple_of(m * mine, 128), mine)
                grad = contract(low_in[:, place], right, 0, 0).astype(LOW)
                for i in range(mine // tall):
                    z, a, s = spot_of(m * (mine // tall) + i, core)
                    parts[kind][k, z, a, s] = grad[i * tall : (i + 1) * tall]

            if fused:
                Job(kind, k).start()

        @pl.loop(0, pair_count)
        def _(step):
            p = pair_count - 1 - step
            pair_step(step, p)
            grad_qkv[p, :, pl.ds(2 * PAIR, PAIR)] = value_sum[...].astype(LOW)

            @pl.when(p > 0)
            def _():
                grad_qkv[p, :, pl.ds(PAIR, PAIR)] = key_sum[...].astype(LOW)
                weights_into("attn", p - 1, grad_qkv[p])

            steps_when(step == 0, "up1 gather", "out turn", "down cross")
            steps_when(step == 1, "attn2 turn", "out gather", "up0 close")

        keep_all = lanes_below((length, PAIR), HEAD)
        second_head = jnp.where(
            keep_all,
            pltpu.roll(grad_qkv[0, :, pl.ds(0, PAIR)].astype(FULL), HEAD, 1),
            key_sum[...],
        )
        weights_into(
            "early",
            0,
            jnp.concatenate(
                [second_head.astype(LOW), grad_qkv[0, :, pl.ds(2 * PAIR, PAIR)]], 1
            ),
        )
        slope_load.wait()
        lead_head()
        grad_qkv[0, :, pl.ds(PAIR, PAIR)] = key_sum[...].astype(LOW)
        first_head = jnp.where(
            keep_all,
            grad_qkv[0, :, pl.ds(0, PAIR)].astype(FULL),
            pltpu.roll(key_sum[...], HEAD, 1),
        )
        weights_into("lead", 0, first_head.astype(LOW))

        for one in weight_loads:
            one.wait()

        def in_part(here):
            joined = jnp.concatenate([grad_qkv[p, here, :] for p in range(pair_count)], 1)
            return contract(joined, weight_in[...], 1, 1)

        @pl.loop(0, tiles)
        def _(i):
            part = in_part(rows_of(lax.rem(other * 2 + i, tiles) * TILE, TILE))

            @pl.when(i < 2)
            def _():
                stage[tile_rows(i), :] = part.astype(LOW)
                in_back(i).start()

            @pl.when(i >= 2)
            def _():
                fades[tile_rows(i - 2), pl.ds(0, width)] = part

            steps_when(i == 1, "attn1 turn", "attn2 gather")
            steps_when(i == 3, "early turn", "attn1 gather", "down close")

        steps("lead turn")
        for i in range(2):
            mid_far(i).wait_send()

        @pl.loop(0, 2)
        def _(i):
            here = tile_rows(i)
            in_back(i).wait_recv()
            grad = fades[here, pl.ds(0, width)] + catch_mid[here, :].astype(FULL)
            unit, inverse = layer_norm(tokens[here, :].astype(FULL))
            vec_sums[0:1, :] += jnp.sum(grad * unit, 0, keepdims=True)
            vec_sums[1:2, :] += jnp.sum(grad, 0, keepdims=True)
            scaled = grad * flat(gain_in)
            low_mid[here, :] = (
                grad_resid[here, :]
                + inverse
                * (
                    scaled
                    - jnp.mean(scaled, -1, keepdims=True)
                    - unit * jnp.mean(scaled * unit, -1, keepdims=True)
                )
            ).astype(LOW)

        in_put.start()
        for i in range(2):
            in_back(i).wait_send()

    pl.run_scoped(
        attention,
        pltpu.VMEM((tiles * (tiles + 1) // 2, TILE, TILE), LOW),
        pltpu.VMEM((length, length), FULL),
        pltpu.VMEM((length, PAIR), FULL),
        pltpu.VMEM((length, PAIR), FULL),
        pltpu.VMEM((length, 1), FULL),
        pltpu.VMEM((pair_count, length, mine), LOW),
        pltpu.VMEM((width, 3 * mine), LOW),
    )

    if not fused:
        for kind in KINDS[:-1]:
            one = pltpu.make_async_copy(parts[kind], results[kind], load_sems.at[0])
            one.start()
            one.wait()
        one = pltpu.make_async_copy(vec_sums, results["vec"], load_sems.at[0])
        one.start()
        one.wait()
    else:
        sums = vec_sums[...]
        tall = width // COUNT
        for rank in range(COUNT):
            z, a, s = spot_of(rank, core)
            shifted = pltpu.roll(sums, width - rank * tall, 1) if rank else sums
            parts["vec"][0, z, a, s] = shifted[:, :128]
    steps("vec start", "early gather")

    def out_part(here):
        return contract(hidden_low[0, here, :], weight_down[0], 1, 0) + contract(
            hidden_low[1, here, :], weight_down[1], 1, 0
        )

    @pl.loop(0, tiles)
    def _(i):
        part = out_part(rows_of(lax.rem(other * 2 + i, tiles) * TILE, TILE))

        @pl.when(i < 2)
        def _():
            stage_far[tile_rows(i), :] = part.astype(LOW)
            out_back(i).start()

        @pl.when(i >= 2)
        def _():
            resid[tile_rows(i - 2), :] += part

        steps_when(i == 0, "lead gather", "up1 close")
        steps_when(i == 1, "vec gather", "out close", "attn2 close")
        steps_when(i == 2, "attn1 close")

    steps("early close", "lead close", "down store", "up0 store", "up1 store")

    @pl.loop(0, 2)
    def _(i):
        here = tile_rows(i)
        out_back(i).wait_recv()
        low_mid[rows_of(half + i * TILE, TILE), :] = (
            resid[here, :] + catch_out[here, :].astype(FULL)
        ).astype(LOW)

    out_put.start()
    steps("out store", "attn2 store", "attn1 store", "early store", "vec close")
    steps("lead store", "vec store")
    if fused:
        for job in jobs.values():
            job.drain()
    in_put.wait()
    out_put.wait()
    g_far.wait_send()
    give_out.wait_send()
    for i in range(2):
        give_down(i).wait_send()
        for one in (dz_far, out_back):
            one(i).wait_send()


def finish(fused, tokens, cotangent, gain_in, gain_mid, shift_mid, forward, weights):
    low_in, queries, keys, values, probs, slopes, heads, heads_far = forward
    half, width = tokens.shape
    length, mine = 2 * half, width // 2
    hidden = weights[-1].shape[0]
    pairs, tiles = mine // PAIR, length // TILE
    shapes = block_shapes(width, hidden)
    long, wide, deep = GRID
    anywhere = pl.BlockSpec(memory_space=pl.ANY)
    local = pl.BlockSpec(memory_space=pltpu.VMEM)
    outs = [jax.ShapeDtypeStruct((half, width), LOW)] * 2
    out_specs = [anywhere] * 2
    for kind in KINDS:
        shape, kept = shapes[kind]
        if fused:
            outs.append(jax.ShapeDtypeStruct((FAN[kind], 2) + shape, kept))
            out_specs.append(local)
        elif kind == "vec":
            outs.append(jax.ShapeDtypeStruct((8, width), FULL))
            out_specs.append(anywhere)
        else:
            outs.append(jax.ShapeDtypeStruct((FAN[kind],) + GRID + shape, kept))
            out_specs.append(anywhere)
    scratch = [
        pltpu.VMEM((length, width), LOW),
        pltpu.VMEM((width, width), LOW),
        pltpu.VMEM((pairs, length, PAIR), LOW),
        pltpu.VMEM((pairs, half, PAIR), LOW),
        pltpu.VMEM((half, width), FULL),
        pltpu.VMEM((length, width), LOW),
        pltpu.VMEM((half, width), FULL),
        pltpu.VMEM((length, width), LOW),
        pltpu.VMEM((pairs, length, PAIR), LOW),
        pltpu.VMEM((length, width), LOW),
        pltpu.VMEM((pairs, length, PAIR), LOW),
        pltpu.VMEM((pairs, length, PAIR), LOW),
        pltpu.VMEM((pairs, length, PAIR), LOW),
    ]
    scratch += [pltpu.VMEM(((t + 1) * TILE, 2 * TILE), LOW) for t in range(tiles)]
    corners = tiles * (tiles + 1) // 2
    scratch += [pltpu.VMEM((corners, TILE, TILE), LOW)] * 2
    scratch += [pltpu.VMEM((half, width), LOW)] * 4
    block = hidden // 4
    scratch += [pltpu.VMEM((2, block, width), LOW), pltpu.VMEM((2, length, block), LOW)]
    scratch += [
        pltpu.VMEM((2, wide, deep) + shapes["down"][0], LOW),
        pltpu.VMEM((2, wide, deep) + shapes["out"][0], LOW),
        pltpu.VMEM((8, width), FULL),
    ]
    scratch += [pltpu.VMEM((FAN[kind],) + GRID + shapes[kind][0], shapes[kind][1]) for kind in KINDS]
    dma = pltpu.SemaphoreType.DMA
    if fused:
        leads = {kind: ((long, deep), (long,), (long - 1,), ()) for kind in KINDS}
        leads["down"] = ((long, deep), (long - 1, deep), (), ())
        leads["vec"] = ((3, long), (), (long - 1,), ())
        for step in range(4):
            scratch += [
                pltpu.VMEM((FAN[kind],) + leads[kind][step] + shapes[kind][0], shapes[kind][1])
                for kind in KINDS
            ]
        scratch += [dma((long,))] * 2 + [dma((long - 1,))] * 2 + [dma((1,))] * 4
        for kind in KINDS[1:]:
            fan = FAN[kind]
            count = 3 if kind == "vec" else fan
            scratch += [dma((count,))] * 4 + [dma((fan, long - 1))] * 2 + [dma((fan,))] * 2
    scratch += [dma((17 + 3 * pairs,)), dma((2,))]
    scratch += [dma((2, 2))] * 6
    scratch += [dma((2,)), dma((2, tiles)), dma((tiles,))]
    return pl.pallas_call(
        functools.partial(finish_kernel, fused),
        out_shape=outs,
        in_specs=[local] + [anywhere] + [local] * 3 + [anywhere] * (4 + tiles + 1 + 2 + 6),
        out_specs=out_specs,
        scratch_shapes=scratch,
        compiler_params=pltpu.CompilerParams(
            collective_id=0, has_side_effects=True, vmem_limit_bytes=VMEM_LIMIT
        ),
        name="finish",
    )(
        tokens,
        cotangent,
        gain_in,
        gain_mid,
        shift_mid,
        low_in,
        queries,
        keys,
        values,
        *probs,
        slopes,
        heads,
        heads_far,
        *weights,
    )

def deliver_kernel(
    output_in,
    grad_in,
    share_in,
    down,
    up,
    out,
    attn,
    early,
    lead,
    vec,
    output,
    input_grad,
    share,
    *grads,
):
    output[...] = output_in[...]
    input_grad[...] = grad_in[...]
    share[...] = share_in[0:1, :]
    g_query, g_key, g_value, g_out, g_up, g_down, *g_vecs = grads
    tall, mine = out.shape[2:]
    for k in range(2):
        g_down[:, k * mine : (k + 1) * mine] = down[0, k].astype(FULL)
        g_out[:, k * mine : (k + 1) * mine] = out[0, k].astype(FULL)
        for b in range(2):
            g_up[:, (2 * k + b) * 2 * mine : (2 * k + b + 1) * 2 * mine] = up[b, k].astype(FULL)
        for p in range(attn.shape[0]):
            for place, target in enumerate((g_query, g_key, g_value)):
                target[:, k * mine + (p + 1) * PAIR : k * mine + (p + 2) * PAIR] = attn[
                    p, k, :, place * PAIR : (place + 1) * PAIR
                ].astype(FULL)
        start = k * mine
        ones, twos = lead[0, k].astype(FULL), early[0, k].astype(FULL)
        keep = lanes_below(ones.shape, HEAD)
        seconds = twos[:, :PAIR]
        g_query[:, start : start + PAIR] = jnp.where(keep, ones, pltpu.roll(seconds, HEAD, 1))
        g_key[:, start : start + PAIR] = jnp.where(keep, pltpu.roll(ones, HEAD, 1), seconds)
        g_value[:, start : start + PAIR] = twos[:, PAIR:]
    sums = vec[0, 0] + vec[0, 1]
    for i, target in enumerate(g_vecs):
        target[...] = sums[i, :tall]


def deliver(output, input_grad, shares, down, up, out, attn, early, lead, vec):
    tall, mine = out.shape[2:]
    width = 2 * mine
    shapes = [(tall, width)] * 4 + [(tall, 2 * up.shape[3] * 2), (down.shape[2], width)]
    shapes += [(tall,)] * 4
    return pl.pallas_call(
        deliver_kernel,
        out_shape=[
            jax.ShapeDtypeStruct(output.shape, output.dtype),
            jax.ShapeDtypeStruct(input_grad.shape, input_grad.dtype),
            jax.ShapeDtypeStruct((1, shares.shape[1]), FULL),
        ]
        + [jax.ShapeDtypeStruct(shape, FULL) for shape in shapes],
        compiler_params=pltpu.CompilerParams(vmem_limit_bytes=VMEM_LIMIT),
        name="deliver",
    )(output, input_grad, shares, down, up, out, attn, early, lead, vec)


def reduce_plain(parts, rows):
    down, up, out, attn, early, lead, vec = parts
    width = vec.shape[1]

    def scattered(part):
        summed = lax.psum_scatter(part.astype(FULL), "rows", scatter_dimension=0, tiled=True)
        return summed.astype(LOW)

    def joined(part):
        return lax.all_gather(part, "keys", axis=1, tiled=True).astype(FULL)

    def flat_part(part):
        return part.reshape(-1, part.shape[-1])

    ones, twos = scattered(flat_part(lead[0])), scattered(flat_part(early[0]))
    first = [
        jnp.concatenate([ones[:, :HEAD], twos[:, :HEAD]], 1),
        jnp.concatenate([ones[:, HEAD:], twos[:, HEAD:PAIR]], 1),
        twos[:, PAIR:],
    ]
    rest = [scattered(flat_part(attn[p])) for p in range(attn.shape[0])]
    halves = [
        jnp.concatenate([first[i]] + [one[:, i * PAIR : (i + 1) * PAIR] for one in rest], 1)
        for i in range(3)
    ]
    halves.append(scattered(flat_part(out[0])))
    halves.append(jnp.concatenate([scattered(flat_part(up[b])) for b in range(2)], 1))
    halves.append(scattered(flat_part(down[0])))
    sums = lax.psum_scatter(
        lax.psum(vec[:4].T, "keys"), "rows", scatter_dimension=0, tiled=True
    )
    return [joined(one) for one in halves], [sums[:, i] for i in range(4)]


def body(
    rows,
    tokens,
    seg_ids,
    doc_starts,
    gain_in,
    shift_in,
    w_query,
    w_key,
    w_value,
    w_out,
    gain_mid,
    shift_mid,
    w_up,
    w_down,
    out_grad,
):
    fused = rows == COUNT
    own_tokens, own_grad = tokens[0], out_grad[0]
    low_in, queries, keys, values, probs, slopes, heads, heads_far, shares = attend(
        own_tokens, seg_ids, gain_in, shift_in, w_query, w_key, w_value
    )
    output, input_grad, *parts = finish(
        fused,
        own_tokens,
        own_grad,
        gain_in,
        gain_mid,
        shift_mid,
        (low_in, queries, keys, values, probs, slopes, heads, heads_far),
        (w_query, w_key, w_value, w_out, w_up, w_down),
    )
    if fused:
        output, input_grad, shares, *grads = deliver(output, input_grad, shares, *parts)
        grads, vectors = grads[:6], grads[6:]
    else:
        grads, vectors = reduce_plain(parts, rows)
    g_query, g_key, g_value, g_out, g_up, g_down = grads
    return (
        output[None],
        input_grad[None],
        shares[:1],
        vectors[0],
        vectors[1],
        g_query,
        g_key,
        g_value,
        g_out,
        vectors[2],
        vectors[3],
        g_up,
        g_down,
    )


def solution(mesh):
    in_specs = (
        P("rows", "keys", None),
        P("rows", None),
        P("rows", "keys"),
        P(),
        P(),
        P(),
        P(),
        P(),
        P(),
        P(),
        P(),
        P(),
        P(),
        P("rows", "keys", None),
    )
    out_specs = (
        P("rows", "keys", None),
        P("rows", "keys", None),
        P("rows", "keys"),
        P("rows"),
        P("rows"),
        P("rows", None),
        P("rows", None),
        P("rows", None),
        P("rows", None),
        P("rows"),
        P("rows"),
        P("rows", None),
        P("rows", None),
    )
    return jax.shard_map(
        functools.partial(body, mesh.shape["rows"]),
        mesh=mesh,
        in_specs=in_specs,
        out_specs=out_specs,
        check_vma=False,
    )
```

profile of v0, /device:TPU:1, one launch (start us, length us, event | category | flops | bytes accessed | tf_op | source)
XLA Modules:
  0.0 126.0 jit_solution(14790150785989521029)
XLA Ops:
  0.6 31.3 %attend.1 = (bf16[1024,768]{1,0:T(8,128)(2,1)}, bf16[3,1024,128]{2,1,0:T(8,128)(2,1)}, bf16[3,1024,128]{2,1,0:T(8,128)(2,1)}, bf16[3,1024,128]{2,1,0:T(8,128)(2,...) custom-call(bf16[512,768]{1,0:T(8,128)(2,1)} %bitcast.4, ...), custom_call_target="tpu_custom_call" | custom-call | tf_op jit(solution)/shard_map/attend/pallas_call | solution.py:326
  31.9 90.4 %finish.1 = (bf16[512,768]{1,0:T(8,128)(2,1)}, bf16[512,768]{1,0:T(8,128)(2,1)}, bf16[1,2,192,384]{3,2,1,0:T(8,128)(2,1)}, bf16[2,2,48,768]{3,2,1,0:T(8,128)(2,1...) custom-call(bf16[512,768]{1,0:T(8,128)(2,1)} %bitcast.5, ...), custom_call_target="tpu_custom_call" | custom-call | tf_op jit(solution)/shard_map/finish/pallas_call | solution.py:1322
  122.4 3.4 %deliver.1 = (bf16[512,768]{1,0:T(8,128)(2,1)}, bf16[512,768]{1,0:T(8,128)(2,1)}, f32[1,512]{1,0:T(1,128)}, f32[48,768]{1,0:T(8,128)}, f32[48,768]{1,0:T(8,128)}...) custom-call(bf16[512,768]{1,0:T(8,128)(2,1)} %get-tuple-element.58.o, ...), custom_call_target="tpu_custom_call" | custom-call | tf_op jit(solution)/shard_map/deliver/pallas_call | solution.py:1397
where the time goes:
time: 126 us
  Pallas kernels  125 us (99%)
    pallas_call x1, Pallas kernels, finish(): pl.pallas_call(functools.partial(finish_kernel, fused), out_shape=outs, i...  90.4 us
    pallas_call x1, Pallas kernels, attend(): pl.pallas_call(attend_kernel, out_shape=outs, in_specs=[anywhere] + [loca...  31.3 us
    pallas_call x1, Pallas kernels, deliver(): pl.pallas_call(deliver_kernel, out_shape=[jax.ShapeDtypeStruct(output.sha...  3.44 us

commit v1 on v0

--- a/solution.py
+++ b/solution.py
@@ -180,27 +180,22 @@
         one.start()
 
     spots = (
-        lax.broadcasted_iota(jnp.int32, (TILE, 2 * TILE), 0),
-        lax.broadcasted_iota(jnp.int32, (TILE, 2 * TILE), 1),
-    )
-    pairs = (
         lax.broadcasted_iota(jnp.int32, (2 * TILE, 2 * TILE), 0),
         lax.broadcasted_iota(jnp.int32, (2 * TILE, 2 * TILE), 1),
     )
-    earlier = jnp.where(pairs[0] < pairs[1], 1.0, 0.0).astype(LOW)
+    earlier = jnp.where(spots[0] < spots[1], 1.0, 0.0).astype(LOW)
     running[...] = jnp.zeros_like(running)
     numerator[...] = jnp.zeros_like(numerator)
     pairs_seen[...] = jnp.zeros_like(pairs_seen)
 
-    @pl.loop(0, (tiles // 2) * (tiles // 2 + 1))
+    @pl.loop(0, (tiles // 2) * (tiles // 2 + 1) // 2)
     def _(step):
-        wide = sum((step >= n * (n + 1)).astype(jnp.int32) for n in range(1, tiles // 2))
-        k = step - wide * (wide + 1)
-        rows, span = rows_of(k * TILE, TILE), rows_of(wide * 2 * TILE, 2 * TILE)
+        wide, k = corner(step, tiles // 2)
+        rows, span = rows_of(k * 2 * TILE, 2 * TILE), rows_of(wide * 2 * TILE, 2 * TILE)
         scores = contract(lead_key[rows, :], lead_query[span, :], 1, 1)
         repeat = 2 * TILE // 128
         same = jnp.concatenate([seg_cols[rows, :]] * repeat, 1) == seg[:, span].astype(FULL)
-        ahead = spots[1] - spots[0] + (2 * wide - k) * TILE
+        ahead = spots[1] - spots[0] + (wide - k) * 2 * TILE
         later = same & (ahead > 0)
         allowed = same & (ahead >= 0)
         select = jnp.where(later, jnp.concatenate([free_cols[rows, :]] * repeat, 1), 0.0)
@@ -208,11 +203,14 @@
         chosen = select * (jnp.maximum(level, 0.0) + jnp.log(1.0 + jnp.exp(-jnp.abs(level))))
         slope = (select * (0.5 + 0.5 * jnp.tanh(0.5 * level))).astype(LOW)
 
-        @pl.when(k <= 2 * wide)
+        slopes[wide * (2 * wide + 1) + 2 * k] = slope[:TILE, :TILE]
+
+        @pl.when(k < wide)
         def _():
-            slopes[wide * (2 * wide + 1) + k] = slope[:, :TILE]
-
-        slopes[(2 * wide + 1) * (wide + 1) + k] = slope[:, TILE:]
+            slopes[wide * (2 * wide + 1) + 2 * k + 1] = slope[TILE:, :TILE]
+
+        slopes[(2 * wide + 1) * (wide + 1) + 2 * k] = slope[:TILE, TILE:]
+        slopes[(2 * wide + 1) * (wide + 1) + 2 * k + 1] = slope[TILE:, TILE:]
         high = chosen.astype(LOW)
         rest = (chosen - high.astype(FULL)).astype(LOW)
         total = (
@@ -414,6 +412,8 @@
         for kind in KINDS[1:]:
             for stage_name in "1234":
                 sems[kind + stage_name] = take(2)
+        for kind in KINDS:
+            sems[kind + "5"] = take(1)
     (load_sems, g_sems, mid_sems, dz_sems, a_sems, b_sems, c_sems, pd_sems, po_sems, df_sems, prob_sems) = take(11)
 
     long, wide, deep = GRID
@@ -534,11 +534,19 @@
             )
             self.last_copy().start()
 
+        def puts(self):
+            kind, k = self.kind, self.k
+            own_part = parts[kind].at[k, slow, first, second]
+            sem = sems[kind + "5"]
+            return [
+                pltpu.make_async_copy(own_part, results[kind].at[k, core], sem.at[k, 0]),
+                pltpu.make_async_copy(pair[kind].at[k], results[kind].at[k, other], sem.at[k, 1]),
+            ]
+
         def store(self):
             self.last_copy().wait_recv()
-            kind, k = self.kind, self.k
-            results[kind][k, core] = parts[kind][k, slow, first, second]
-            results[kind][k, other] = pair[kind][k]
+            for one in self.puts():
+                one.start()
 
         def drain(self):
             self.first_copy().wait_send()
@@ -546,6 +554,8 @@
             for one in self.third_copies():
                 one.wait_send()
             self.last_copy().wait_send()
+            for one in self.puts():
+                one.wait()
 
     class Down(Job):
         def near_copy(self, z):
@@ -621,6 +631,8 @@
                 self.slow_copy(step).wait_send()
             self.next_copy().wait_send()
             self.last_copy().wait_send()
+            for one in self.puts():
+                one.wait()
 
     class Vectors(Job):
         def first_copies(self):
@@ -658,6 +670,8 @@
             for one in self.first_copies() + self.third_copies():
                 one.wait_send()
             self.last_copy().wait_send()
+            for one in self.puts():
+                one.wait()
 
     def steps(*names):
         if fused:
@@ -772,9 +786,9 @@
             low_mid[place, :] = (unit * flat(gain_mid) + flat(shift_mid)).astype(LOW)
 
         pl.semaphore_wait(barrier, len(peers))
-        g_far.start()
         for i in range(2):
             mid_far(i).start()
+        g_far.start()
 
         for one in up_loads + down_loads + [g_load]:
             one.wait()
@@ -796,13 +810,9 @@
                 grad_up[b, here, :] = slope.astype(LOW)
                 if fused:
 
-                    @pl.when((b == 1) & (i == 0))
+                    @pl.when((b == 1) & (i == 3))
                     def _():
                         down.turn_at(core * 2)
-
-                    @pl.when((b == 1) & (i == 2))
-                    def _():
-                        down.turn_at(other * 2)
 
             @pl.when(b == 0)
             def _():
@@ -832,13 +842,17 @@
                 back = contract(grads_all[here, :], weight_down[b], 1, 1)
                 grad_up[b, here, :] = (back * grad_up[b, here, :].astype(FULL)).astype(LOW)
 
-                @pl.when(i == 1)
+                @pl.when(i == 3)
                 def _():
                     give_down(b).wait_recv()
                     if fused:
                         down.start_at(other * 2 + b)
 
-                steps_when((b == 1) & (i == 2), "up0 turn")
+                if fused:
+
+                    @pl.when((b == 1) & (i == 1))
+                    def _():
+                        down.turn_at(other * 2)
 
             @pl.loop(0, 2)
             def _(m):
@@ -871,15 +885,7 @@
             def _():
                 grad_resid[tile_rows(i - 2), :] = part
 
-            if fused:
-
-                @pl.when(i == 1)
-                def _():
-                    down.turn_at(core * 2 + 1)
-
-        if fused:
-            down.turn_at(other * 2 + 1)
-        steps("up0 gather")
+            steps_when(i == 1, "up0 turn")
 
         @pl.loop(0, 2)
         def _(i):
@@ -901,6 +907,8 @@
 
         for i in range(2):
             mid_back(i).wait_send()
+        if fused:
+            down.turn_at(core * 2 + 1)
 
     def give_down(b):
         return remote(
@@ -973,8 +981,8 @@
         give_out.start()
         for one in late_loads:
             one.wait()
-        give_out.wait_recv()
-        steps("out start", "up1 turn")
+        if fused:
+            down.turn_at(other * 2 + 1)
 
         keep = lanes_below((TILE, PAIR), HEAD)
         spots = (
@@ -1040,6 +1048,10 @@
                 @pl.when(step < pair_count - 1)
                 def _():
                     prob_load(p - 1, t).start()
+
+                if t == tiles - 1:
+                    steps_when(step == 1, "up1 turn")
+                    steps_when(step == 2, "out turn", "down cross", "up1 gather")
 
                 @pl.when((step == pair_count - 1) & (core == 1))
                 def _():
@@ -1099,8 +1111,11 @@
                 grad_qkv[p, :, pl.ds(PAIR, PAIR)] = key_sum[...].astype(LOW)
                 weights_into("attn", p - 1, grad_qkv[p])
 
-            steps_when(step == 0, "up1 gather", "out turn", "down cross")
-            steps_when(step == 1, "attn2 turn", "out gather", "up0 close")
+            @pl.when(step == 0)
+            def _():
+                give_out.wait_recv()
+                steps("out start", "up0 gather")
+
 
         keep_all = lanes_below((length, PAIR), HEAD)
         second_head = jnp.where(
@@ -1116,6 +1131,7 @@
             ),
         )
         slope_load.wait()
+        steps("attn2 turn", "up0 close")
         lead_head()
         grad_qkv[0, :, pl.ds(PAIR, PAIR)] = key_sum[...].astype(LOW)
         first_head = jnp.where(
@@ -1145,10 +1161,9 @@
             def _():
                 fades[tile_rows(i - 2), pl.ds(0, width)] = part
 
-            steps_when(i == 1, "attn1 turn", "attn2 gather")
-            steps_when(i == 3, "early turn", "attn1 gather", "down close")
-
-        steps("lead turn")
+            steps_when(i == 1, "attn2 gather", "out gather")
+            steps_when(i == 3, "attn1 turn", "down close")
+
         for i in range(2):
             mid_far(i).wait_send()
 
@@ -1201,7 +1216,7 @@
             z, a, s = spot_of(rank, core)
             shifted = pltpu.roll(sums, width - rank * tall, 1) if rank else sums
             parts["vec"][0, z, a, s] = shifted[:, :128]
-    steps("vec start", "early gather")
+    steps("vec start", "early turn")
 
     def out_part(here):
         return contract(hidden_low[0, here, :], weight_down[0], 1, 0) + contract(
@@ -1221,11 +1236,12 @@
         def _():
             resid[tile_rows(i - 2), :] += part
 
-        steps_when(i == 0, "lead gather", "up1 close")
-        steps_when(i == 1, "vec gather", "out close", "attn2 close")
-        steps_when(i == 2, "attn1 close")
-
-    steps("early close", "lead close", "down store", "up0 store", "up1 store")
+        steps_when(i == 0, "lead turn", "attn1 gather", "up1 close")
+        steps_when(i == 1, "early gather")
+        steps_when(i == 2, "vec gather", "out close")
+        steps_when(i == 3, "lead gather", "attn2 close")
+
+    steps("down store", "up0 store", "up1 store")
 
     @pl.loop(0, 2)
     def _(i):
@@ -1236,8 +1252,8 @@
         ).astype(LOW)
 
     out_put.start()
-    steps("out store", "attn2 store", "attn1 store", "early store", "vec close")
-    steps("lead store", "vec store")
+    steps("attn1 close", "early close", "vec close", "lead close")
+    steps("out store", "attn2 store", "attn1 store", "early store", "vec store", "lead store")
     if fused:
         for job in jobs.values():
             job.drain()
@@ -1267,7 +1283,7 @@
         shape, kept = shapes[kind]
         if fused:
             outs.append(jax.ShapeDtypeStruct((FAN[kind], 2) + shape, kept))
-            out_specs.append(local)
+            out_specs.append(anywhere)
         elif kind == "vec":
             outs.append(jax.ShapeDtypeStruct((8, width), FULL))
             out_specs.append(anywhere)
@@ -1316,6 +1332,7 @@
             fan = FAN[kind]
             count = 3 if kind == "vec" else fan
             scratch += [dma((count,))] * 4 + [dma((fan, long - 1))] * 2 + [dma((fan,))] * 2
+        scratch += [dma((FAN[kind], 2)) for kind in KINDS]
     scratch += [dma((17 + 3 * pairs,)), dma((2,))]
     scratch += [dma((2, 2))] * 6
     scratch += [dma((2,)), dma((2, tiles)), dma((tiles,))]
@@ -1346,65 +1363,79 @@
         *weights,
     )
 
-def deliver_kernel(
-    output_in,
-    grad_in,
-    share_in,
-    down,
-    up,
-    out,
-    attn,
-    early,
-    lead,
-    vec,
-    output,
-    input_grad,
-    share,
-    *grads,
-):
-    output[...] = output_in[...]
-    input_grad[...] = grad_in[...]
-    share[...] = share_in[0:1, :]
-    g_query, g_key, g_value, g_out, g_up, g_down, *g_vecs = grads
+def deliver_kernel(count, *refs):
+    refs, (load_sems, put_sems) = refs[:-2], refs[-2:]
+    targets = refs[count : (len(refs) - 2 * count + 2) // 2 + count]
+    sources, held = refs[:count], refs[count + len(targets) : 2 * count + len(targets)]
+    made = refs[2 * count + len(targets) :]
+    loads = [
+        pltpu.make_async_copy(source, target, load_sems.at[i])
+        for i, (source, target) in enumerate(zip(sources, held))
+    ]
+    for one in loads[2:] + loads[:2]:
+        one.start()
+    puts = [
+        pltpu.make_async_copy(source, target, put_sems.at[i])
+        for i, (source, target) in enumerate(zip(held[:2] + made, targets))
+    ]
+    for one in loads[2:]:
+        one.wait()
+    share_in, down, up, out, attn, early, lead, vec = held[2:]
+    share, g_query, g_key, g_value, g_out, g_up, g_down, *g_vecs = made
     tall, mine = out.shape[2:]
     for k in range(2):
-        g_down[:, k * mine : (k + 1) * mine] = down[0, k].astype(FULL)
-        g_out[:, k * mine : (k + 1) * mine] = out[0, k].astype(FULL)
         for b in range(2):
             g_up[:, (2 * k + b) * 2 * mine : (2 * k + b + 1) * 2 * mine] = up[b, k].astype(FULL)
+    puts[7].start()
+    for k in range(2):
+        g_down[:, k * mine : (k + 1) * mine] = down[0, k].astype(FULL)
+    puts[8].start()
+    for i in range(2):
+        loads[i].wait()
+        puts[i].start()
+    for k in range(2):
+        start = k * mine
+        g_out[:, start : start + mine] = out[0, k].astype(FULL)
         for p in range(attn.shape[0]):
             for place, target in enumerate((g_query, g_key, g_value)):
-                target[:, k * mine + (p + 1) * PAIR : k * mine + (p + 2) * PAIR] = attn[
+                target[:, start + (p + 1) * PAIR : start + (p + 2) * PAIR] = attn[
                     p, k, :, place * PAIR : (place + 1) * PAIR
                 ].astype(FULL)
-        start = k * mine
         ones, twos = lead[0, k].astype(FULL), early[0, k].astype(FULL)
         keep = lanes_below(ones.shape, HEAD)
         seconds = twos[:, :PAIR]
         g_query[:, start : start + PAIR] = jnp.where(keep, ones, pltpu.roll(seconds, HEAD, 1))
         g_key[:, start : start + PAIR] = jnp.where(keep, pltpu.roll(ones, HEAD, 1), seconds)
         g_value[:, start : start + PAIR] = twos[:, PAIR:]
+    share[...] = share_in[0:1, :]
     sums = vec[0, 0] + vec[0, 1]
     for i, target in enumerate(g_vecs):
         target[...] = sums[i, :tall]
-
-
-def deliver(output, input_grad, shares, down, up, out, attn, early, lead, vec):
+    for one in puts[2:7] + puts[9:]:
+        one.start()
+    for one in puts:
+        one.wait()
+
+
+def deliver(*arrays):
+    output, _, shares, down, up, out = arrays[:6]
     tall, mine = out.shape[2:]
     width = 2 * mine
-    shapes = [(tall, width)] * 4 + [(tall, 2 * up.shape[3] * 2), (down.shape[2], width)]
-    shapes += [(tall,)] * 4
+    shapes = [(1, shares.shape[1])] + [(tall, width)] * 4
+    shapes += [(tall, 2 * up.shape[3] * 2), (down.shape[2], width)] + [(tall,)] * 4
+    anywhere = pl.BlockSpec(memory_space=pl.ANY)
     return pl.pallas_call(
-        deliver_kernel,
-        out_shape=[
-            jax.ShapeDtypeStruct(output.shape, output.dtype),
-            jax.ShapeDtypeStruct(input_grad.shape, input_grad.dtype),
-            jax.ShapeDtypeStruct((1, shares.shape[1]), FULL),
-        ]
+        functools.partial(deliver_kernel, len(arrays)),
+        out_shape=[jax.ShapeDtypeStruct(output.shape, output.dtype)] * 2
         + [jax.ShapeDtypeStruct(shape, FULL) for shape in shapes],
+        in_specs=[anywhere] * len(arrays),
+        out_specs=[anywhere] * (2 + len(shapes)),
+        scratch_shapes=[pltpu.VMEM(one.shape, one.dtype) for one in arrays]
+        + [pltpu.VMEM(shape, FULL) for shape in shapes]
+        + [pltpu.SemaphoreType.DMA((len(arrays),)), pltpu.SemaphoreType.DMA((2 + len(shapes),))],
         compiler_params=pltpu.CompilerParams(vmem_limit_bytes=VMEM_LIMIT),
         name="deliver",
-    )(output, input_grad, shares, down, up, out, attn, early, lead, vec)
+    )(*arrays)
 
 
 def reduce_plain(parts, rows):

time: 126 us -> 118 us (0.937)
  Pallas kernels: 125 us -> 117 us
    pallas_call x1, Pallas kernels: 90.4 us -> 83.4 us  [finish(): pl.pallas_call(functools.partial(finish_kernel, fused), out_shape=outs, i...]
where the time goes in v1:
time: 118 us
  Pallas kernels  117 us (99%)
    pallas_call x1, Pallas kernels, finish(): pl.pallas_call(functools.partial(finish_kernel, fused), out_shape=outs, i...  83.4 us
    pallas_call x1, Pallas kernels, attend(): pl.pallas_call(attend_kernel, out_shape=outs, in_specs=[anywhere] + [loca...  30.2 us
    pallas_call x1, Pallas kernels, deliver(): pl.pallas_call(functools.partial(deliver_kernel, len(arrays)), out_shape=...  3.11 us

profile of v1, /device:TPU:1, one launch (start us, length us, event | category | flops | bytes accessed | tf_op | source)
XLA Modules:
  0.0 117.5 jit_solution(784311016907843668)
XLA Ops:
  0.6 30.2 %attend.1 = (bf16[1024,768]{1,0:T(8,128)(2,1)}, bf16[3,1024,128]{2,1,0:T(8,128)(2,1)}, bf16[3,1024,128]{2,1,0:T(8,128)(2,1)}, bf16[3,1024,128]{2,1,0:T(8,128)(2,...) custom-call(bf16[512,768]{1,0:T(8,128)(2,1)} %bitcast.4, ...), custom_call_target="tpu_custom_call" | custom-call | tf_op jit(solution)/shard_map/attend/pallas_call | solution.py:324
  30.9 83.4 %finish.1 = (bf16[512,768]{1,0:T(8,128)(2,1)}, bf16[512,768]{1,0:T(8,128)(2,1)}, bf16[1,2,192,384]{3,2,1,0:T(8,128)(2,1)}, bf16[2,2,48,768]{3,2,1,0:T(8,128)(2,1...) custom-call(bf16[512,768]{1,0:T(8,128)(2,1)} %bitcast.5, ...), custom_call_target="tpu_custom_call" | custom-call | tf_op jit(solution)/shard_map/finish/pallas_call | solution.py:1339
  114.2 3.1 %deliver.1 = (bf16[512,768]{1,0:T(8,128)(2,1)}, bf16[512,768]{1,0:T(8,128)(2,1)}, f32[1,512]{1,0:T(1,128)}, f32[48,768]{1,0:T(8,128)}, f32[48,768]{1,0:T(8,128)}...) custom-call(bf16[512,768]{1,0:T(8,128)(2,1)} %get-tuple-element.58.r, ...), custom_call_target="tpu_custom_call" | custom-call | tf_op jit(solution)/shard_map/deliver/pallas_call | solution.py:1427

commit v2 on v1

--- a/solution.py
+++ b/solution.py
@@ -75,6 +75,7 @@
     slopes_out,
     heads_out,
     other_out,
+    scales_out,
     share_out,
     all_tokens,
     low_in,
@@ -88,6 +89,8 @@
     slopes,
     penalty,
     heads,
+    scales,
+    scale_cols,
     seg_cols,
     free_cols,
     running,
@@ -184,6 +187,7 @@
         lax.broadcasted_iota(jnp.int32, (2 * TILE, 2 * TILE), 1),
     )
     earlier = jnp.where(spots[0] < spots[1], 1.0, 0.0).astype(LOW)
+    scales[...] = jnp.zeros_like(scales)
     running[...] = jnp.zeros_like(running)
     numerator[...] = jnp.zeros_like(numerator)
     pairs_seen[...] = jnp.zeros_like(pairs_seen)
@@ -248,29 +252,36 @@
             count = (t + 1) * TILE
             span = pl.ds(t * TILE, TILE)
             query = queries[p, span, :]
-            outs = []
-            for h in range(2):
-                masked = jnp.where(keep == (h == 0), query, LOW(0.0))
-                logits = (
-                    contract(keys[p, pl.ds(0, count), :], masked, 1, 1)
-                    - penalty[pl.ds(0, count), span]
-                )
-                scaled = jnp.exp(logits - jnp.max(logits, 0, keepdims=True))
-                prob = (scaled * (1.0 / jnp.sum(scaled, 0, keepdims=True))).astype(LOW)
-                probs[t][p, :, pl.ds(h * TILE, TILE)] = prob
-                out = contract(values[p, pl.ds(0, count), :], prob, 0, 0)
-                outs.append(out[h * HEAD : (h + 1) * HEAD, :])
-            heads[p, span, :] = jnp.concatenate(outs, 0).T.astype(LOW)
+            both = jnp.concatenate(
+                [jnp.where(keep, query, LOW(0.0)), jnp.where(keep, LOW(0.0), query)], 0
+            )
+            fine = penalty[pl.ds(0, count), span]
+            logits = contract(keys[p, pl.ds(0, count), :], both, 1, 1) - jnp.concatenate(
+                [fine, fine], 1
+            )
+            scaled = jnp.exp(logits - jnp.max(logits, 0, keepdims=True))
+            prob = scaled.astype(LOW)
+            probs[t][p] = prob
+            scale = 1.0 / jnp.sum(scaled, 0, keepdims=True)
+            scales[pl.ds(2 * p, 1), span] = scale[:, :TILE]
+            scales[pl.ds(2 * p + 1, 1), span] = scale[:, TILE:]
+            out = contract(values[p, pl.ds(0, count), :], prob, 0, 0) * scale
+            out = jnp.concatenate([out[:HEAD, :TILE], out[HEAD:, TILE:]], 0)
+            heads[p, span, :] = out.T.astype(LOW)
+        for t in range(tiles):
             put_probs(p, t).start()
         send_heads(p).start()
 
+    scale_cols[...] = scales[...].T
+    scale_put = pltpu.make_async_copy(scale_cols, scales_out, out_sems.at[6])
+    scale_put.start()
     last = pltpu.make_async_copy(heads, heads_out, out_sems.at[5])
     last.start()
     for p in range(pair_count):
         send_heads(p).wait()
         for t in range(tiles):
             put_probs(p, t).wait()
-    for one in puts + [slope_put, last]:
+    for one in puts + [slope_put, scale_put, last]:
         one.wait()
     exchange.wait_send()
 
@@ -290,11 +301,12 @@
         jax.ShapeDtypeStruct((corners, TILE, TILE), LOW),
         jax.ShapeDtypeStruct((pairs, length, PAIR), LOW),
         jax.ShapeDtypeStruct((pairs, half, PAIR), LOW),
+        jax.ShapeDtypeStruct((length, 128), FULL),
         jax.ShapeDtypeStruct((8, half), FULL),
     ]
     anywhere = pl.BlockSpec(memory_space=pl.ANY)
     local = pl.BlockSpec(memory_space=pltpu.VMEM)
-    out_specs = [anywhere] * 4 + [[anywhere] * tiles, anywhere, anywhere, anywhere, local]
+    out_specs = [anywhere] * 4 + [[anywhere] * tiles, anywhere, anywhere, anywhere, anywhere, local]
     scratch = [
         pltpu.VMEM((length, width), LOW),
         pltpu.VMEM((length, width), LOW),
@@ -308,6 +320,8 @@
         pltpu.VMEM((corners, TILE, TILE), LOW),
         pltpu.VMEM((length, length), FULL),
         pltpu.VMEM((pairs, length, PAIR), LOW),
+        pltpu.VMEM((128, length), FULL),
+        pltpu.VMEM((length, 128), FULL),
         pltpu.VMEM((length, 128), FULL),
         pltpu.VMEM((length, 128), FULL),
         pltpu.VMEM((length, 1), FULL),
@@ -318,7 +332,7 @@
         pltpu.SemaphoreType.DMA((pairs,)),
         pltpu.SemaphoreType.DMA((pairs,)),
         pltpu.SemaphoreType.DMA((6,)),
-        pltpu.SemaphoreType.DMA((6,)),
+        pltpu.SemaphoreType.DMA((7,)),
         pltpu.SemaphoreType.DMA((pairs, tiles)),
     ]
     return pl.pallas_call(
@@ -375,7 +389,7 @@
     tokens, cotangent, gain_in, gain_mid, shift_mid = take(5)
     low_in_hbm, query_hbm, key_hbm, value_hbm = take(4)
     prob_hbm, slope_hbm = take(4), take(1)
-    heads_hbm, other_hbm = take(2)
+    heads_hbm, other_hbm, scales_hbm = take(3)
     w_query, w_key, w_value, w_out, w_up, w_down = take(6)
     output, input_grad = take(2)
     results = dict(zip(KINDS, take(len(KINDS))))
@@ -393,7 +407,8 @@
         queries,
         keys,
         values,
-    ) = take(13)
+        scales,
+    ) = take(14)
     probs = take(4)
     share_send, share_recv = take(2)
     stage, stage_far, catch_mid, catch_out = take(4)
@@ -707,8 +722,9 @@
         local(query_hbm, queries, 6),
         local(key_hbm, keys, 7),
         local(value_hbm, values, 8),
+        local(scales_hbm, scales, 14),
     ]
-    for one in out_loads + [g_load]:
+    for one in out_loads:
         one.start()
 
     peers = [partner]
@@ -766,11 +782,10 @@
             local(w_down.at[rows_of((core * 2 + b) * block, block)], weight_down.at[b], 11 + b)
             for b in range(2)
         ]
-        for b in range(2):
-            up_loads[b].start()
-            down_loads[b].start()
         for one in out_loads:
             one.wait()
+        for one in up_loads + [g_load] + down_loads:
+            one.start()
 
         @pl.loop(0, 2)
         def _(i):
@@ -785,12 +800,15 @@
             unit, _ = layer_norm(field)
             low_mid[place, :] = (unit * flat(gain_mid) + flat(shift_mid)).astype(LOW)
 
-        pl.semaphore_wait(barrier, len(peers))
-        for i in range(2):
+            @pl.when(i == 0)
+            def _():
+                pl.semaphore_wait(barrier, len(peers))
+
             mid_far(i).start()
+
         g_far.start()
 
-        for one in up_loads + down_loads + [g_load]:
+        for one in up_loads:
             one.wait()
         for one in late_loads:
             one.start()
@@ -799,10 +817,9 @@
         def _(b):
             @pl.loop(0, tiles)
             def _(i):
-                @pl.when((b == 0) & (i == 2))
+                @pl.when((b == 0) & (i >= 2))
                 def _():
-                    for j in range(2):
-                        mid_far(j).wait_recv()
+                    mid_far(i - 2).wait_recv()
 
                 here = rows_of(lax.rem(core * 2 + i, tiles) * TILE, TILE)
                 value, slope = gelu_parts(contract(low_mid[here, :], weight_up[b], 1, 0))
@@ -816,6 +833,8 @@
 
             @pl.when(b == 0)
             def _():
+                for one in [g_load] + down_loads:
+                    one.wait()
                 g_far.wait_recv()
 
             tall = hidden // COUNT
@@ -934,12 +953,12 @@
         pltpu.VMEM((2, length, block), LOW),
     )
 
-    def prob_load(p, t):
-        return pltpu.make_async_copy(prob_hbm[t].at[p], probs[t], prob_sems.at[t])
+    def prob_load(p, t, slot):
+        return pltpu.make_async_copy(prob_hbm[t].at[p], probs[t].at[slot], prob_sems.at[t, slot])
 
     def attention(slopes, fades, key_sum, value_sum, carry, grad_qkv, weight_in):
         for t in range(tiles):
-            prob_load(pair_count - 1, t).start()
+            prob_load(pair_count - 1, t, 0).start()
         slope_load = local(slope_hbm, slopes, 13)
         weight_loads = []
         for place, source in enumerate((w_query, w_key, w_value)):
@@ -954,10 +973,17 @@
         for one in [slope_load] + weight_loads:
             one.start()
 
+        keep = lanes_below((TILE, PAIR), HEAD)
+        for one in late_loads:
+            one.wait()
+
         def head_grads(here):
-            result = contract(low_resid[here, :], weight_out[pl.ds(0, mine), :], 1, 1).astype(LOW)
+            result = contract(low_resid[here, :], weight_out[pl.ds(0, mine), :], 1, 1)
             for p in range(pair_count):
-                grad_heads[p, here, :] = result[:, p * PAIR : (p + 1) * PAIR]
+                scale = jnp.where(
+                    keep, scales[here, 2 * p : 2 * p + 1], scales[here, 2 * p + 1 : 2 * p + 2]
+                )
+                grad_heads[p, here, :] = (result[:, p * PAIR : (p + 1) * PAIR] * scale).astype(LOW)
 
         @pl.loop(0, tiles)
         def _(i):
@@ -979,12 +1005,9 @@
             _, a, s = spot_of(rank, other)
             stage_out[i // (wide * deep), a, s] = given[i * tall : (i + 1) * tall]
         give_out.start()
-        for one in late_loads:
-            one.wait()
         if fused:
             down.turn_at(other * 2 + 1)
 
-        keep = lanes_below((TILE, PAIR), HEAD)
         spots = (
             lax.broadcasted_iota(jnp.int32, (TILE, TILE), 0),
             lax.broadcasted_iota(jnp.int32, (TILE, TILE), 1),
@@ -1002,37 +1025,43 @@
             )
 
         def pair_step(step, p):
+            slot = lax.rem(step, 2)
+            for t in range(tiles):
+                prob_load(p, t, slot).wait()
+
+            @pl.when(step < pair_count - 1)
+            def _():
+                for t in range(tiles):
+                    prob_load(p - 1, t, 1 - slot).start()
+
             for t in reversed(range(tiles)):
                 count = (t + 1) * TILE
                 span, rows = pl.ds(t * TILE, TILE), pl.ds(0, count)
-                prob_load(p, t).wait()
                 grad_tile = grad_heads[p, span, :]
                 product = (grad_tile.astype(FULL) * heads[p, span, :].astype(FULL)).T
                 query = queries[p, span, :]
-                grads, masked_q, masked_g = [], [], []
-                fade = None
-                for h in range(2):
-                    mask = keep == (h == 0)
-                    masked_g.append(jnp.where(mask, grad_tile, LOW(0.0)))
-                    masked_q.append(jnp.where(mask, query, LOW(0.0)))
-                    delta = jnp.sum(product[h * HEAD : (h + 1) * HEAD, :], 0, keepdims=True)
-                    change = probs[t][:, pl.ds(h * TILE, TILE)].astype(FULL) * (
-                        contract(values[p, rows, :], masked_g[h], 1, 1) - delta
-                    )
-                    fade = change if fade is None else fade + change
-                    grads.append(change.astype(LOW))
-
-                @pl.when(step == 0)
-                def _():
-                    fades[rows, span] = fade
-
-                @pl.when(step > 0)
-                def _():
-                    fades[rows, span] += fade
-
-                both = jnp.concatenate(grads, 1)
-                key_part = contract(both, jnp.concatenate(masked_q, 0), 1, 0)
-                value_part = contract(probs[t][...], jnp.concatenate(masked_g, 0), 1, 0)
+                sides_q = jnp.concatenate(
+                    [jnp.where(keep, query, LOW(0.0)), jnp.where(keep, LOW(0.0), query)], 0
+                )
+                sides_g = jnp.concatenate(
+                    [jnp.where(keep, grad_tile, LOW(0.0)), jnp.where(keep, LOW(0.0), grad_tile)], 0
+                )
+                delta = jnp.concatenate(
+                    [
+                        jnp.sum(product[:HEAD, :], 0, keepdims=True),
+                        jnp.sum(product[HEAD:, :], 0, keepdims=True),
+                    ],
+                    1,
+                )
+                change = probs[t][slot].astype(FULL) * (
+                    contract(values[p, rows, :], sides_g, 1, 1) - delta
+                )
+                fade = change[:, :TILE] + change[:, TILE:]
+                both = change.astype(LOW)
+                fades[rows, span] = jnp.where(step == 0, 0.0, fades[rows, span]) + fade
+
+                key_part = contract(both, sides_q, 1, 0)
+                value_part = contract(probs[t][slot], sides_g, 1, 0)
                 if t == tiles - 1:
                     key_sum[...] = key_part
                     value_sum[...] = value_part
@@ -1045,20 +1074,9 @@
                 )
                 grad_qkv[p, span, pl.ds(0, PAIR)] = (query_part.T * 0.125).astype(LOW)
 
-                @pl.when(step < pair_count - 1)
-                def _():
-                    prob_load(p - 1, t).start()
-
                 if t == tiles - 1:
                     steps_when(step == 1, "up1 turn")
-                    steps_when(step == 2, "out turn", "down cross", "up1 gather")
-
-                @pl.when((step == pair_count - 1) & (core == 1))
-                def _():
-                    share_send[pl.ds(t * (t + 1) // 2, t + 1)] = (
-                        fades[rows, span].astype(LOW).reshape(t + 1, TILE, TILE)
-                    )
-                    fade_send(t).start()
+                    steps_when(step == 2, "attn2 turn", "up1 gather")
 
         def lead_head():
             @pl.when(core == 0)
@@ -1117,6 +1135,17 @@
                 steps("out start", "up0 gather")
 
 
+        @pl.when(core == 1)
+        def _():
+            for t in reversed(range(tiles)):
+                count = (t + 1) * TILE
+                share_send[pl.ds(t * (t + 1) // 2, t + 1)] = (
+                    fades[pl.ds(0, count), pl.ds(t * TILE, TILE)]
+                    .astype(LOW)
+                    .reshape(t + 1, TILE, TILE)
+                )
+                fade_send(t).start()
+
         keep_all = lanes_below((length, PAIR), HEAD)
         second_head = jnp.where(
             keep_all,
@@ -1131,7 +1160,7 @@
             ),
         )
         slope_load.wait()
-        steps("attn2 turn", "up0 close")
+        steps("down cross", "out turn", "attn2 gather", "attn1 turn", "up0 close")
         lead_head()
         grad_qkv[0, :, pl.ds(PAIR, PAIR)] = key_sum[...].astype(LOW)
         first_head = jnp.where(
@@ -1161,8 +1190,8 @@
             def _():
                 fades[tile_rows(i - 2), pl.ds(0, width)] = part
 
-            steps_when(i == 1, "attn2 gather", "out gather")
-            steps_when(i == 3, "attn1 turn", "down close")
+            steps_when(i == 1, "out gather", "early turn", "attn1 gather")
+            steps_when(i == 3, "lead turn")
 
         for i in range(2):
             mid_far(i).wait_send()
@@ -1216,7 +1245,7 @@
             z, a, s = spot_of(rank, core)
             shifted = pltpu.roll(sums, width - rank * tall, 1) if rank else sums
             parts["vec"][0, z, a, s] = shifted[:, :128]
-    steps("vec start", "early turn")
+    steps("vec start", "early gather", "down close")
 
     def out_part(here):
         return contract(hidden_low[0, here, :], weight_down[0], 1, 0) + contract(
@@ -1236,10 +1265,10 @@
         def _():
             resid[tile_rows(i - 2), :] += part
 
-        steps_when(i == 0, "lead turn", "attn1 gather", "up1 close")
-        steps_when(i == 1, "early gather")
-        steps_when(i == 2, "vec gather", "out close")
-        steps_when(i == 3, "lead gather", "attn2 close")
+        steps_when(i == 0, "up1 close", "attn2 close")
+        steps_when(i == 1, "lead gather", "out close")
+        steps_when(i == 2, "vec gather")
+        steps_when(i == 3, "attn1 close")
 
     steps("down store", "up0 store", "up1 store")
 
@@ -1252,7 +1281,7 @@
         ).astype(LOW)
 
     out_put.start()
-    steps("attn1 close", "early close", "vec close", "lead close")
+    steps("early close", "lead close", "vec close")
     steps("out store", "attn2 store", "attn1 store", "early store", "vec store", "lead store")
     if fused:
         for job in jobs.values():
@@ -1268,7 +1297,7 @@
 
 
 def finish(fused, tokens, cotangent, gain_in, gain_mid, shift_mid, forward, weights):
-    low_in, queries, keys, values, probs, slopes, heads, heads_far = forward
+    low_in, queries, keys, values, probs, slopes, heads, heads_far, scales = forward
     half, width = tokens.shape
     length, mine = 2 * half, width // 2
     hidden = weights[-1].shape[0]
@@ -1304,8 +1333,9 @@
         pltpu.VMEM((pairs, length, PAIR), LOW),
         pltpu.VMEM((pairs, length, PAIR), LOW),
         pltpu.VMEM((pairs, length, PAIR), LOW),
+        pltpu.VMEM((length, 128), FULL),
     ]
-    scratch += [pltpu.VMEM(((t + 1) * TILE, 2 * TILE), LOW) for t in range(tiles)]
+    scratch += [pltpu.VMEM((2, (t + 1) * TILE, 2 * TILE), LOW) for t in range(tiles)]
     corners = tiles * (tiles + 1) // 2
     scratch += [pltpu.VMEM((corners, TILE, TILE), LOW)] * 2
     scratch += [pltpu.VMEM((half, width), LOW)] * 4
@@ -1335,11 +1365,11 @@
         scratch += [dma((FAN[kind], 2)) for kind in KINDS]
     scratch += [dma((17 + 3 * pairs,)), dma((2,))]
     scratch += [dma((2, 2))] * 6
-    scratch += [dma((2,)), dma((2, tiles)), dma((tiles,))]
+    scratch += [dma((2,)), dma((2, tiles)), dma((tiles, 2))]
     return pl.pallas_call(
         functools.partial(finish_kernel, fused),
         out_shape=outs,
-        in_specs=[local] + [anywhere] + [local] * 3 + [anywhere] * (4 + tiles + 1 + 2 + 6),
+        in_specs=[local] + [anywhere] + [local] * 3 + [anywhere] * (4 + tiles + 1 + 3 + 6),
         out_specs=out_specs,
         scratch_shapes=scratch,
         compiler_params=pltpu.CompilerParams(
@@ -1360,6 +1390,7 @@
         slopes,
         heads,
         heads_far,
+        scales,
         *weights,
     )
 
@@ -1491,7 +1522,7 @@
 ):
     fused = rows == COUNT
     own_tokens, own_grad = tokens[0], out_grad[0]
-    low_in, queries, keys, values, probs, slopes, heads, heads_far, shares = attend(
+    low_in, queries, keys, values, probs, slopes, heads, heads_far, scales, shares = attend(
         own_tokens, seg_ids, gain_in, shift_in, w_query, w_key, w_value
     )
     output, input_grad, *parts = finish(
@@ -1501,7 +1532,7 @@
         gain_in,
         gain_mid,
         shift_mid,
-        (low_in, queries, keys, values, probs, slopes, heads, heads_far),
+        (low_in, queries, keys, values, probs, slopes, heads, heads_far, scales),
         (w_query, w_key, w_value, w_out, w_up, w_down),
     )
     if fused:

time: 118 us -> 109 us (0.924)
  Pallas kernels: 117 us -> 107 us
    pallas_call x1, Pallas kernels: 30.2 us -> 24.2 us  [attend(): pl.pallas_call(attend_kernel, out_shape=outs, in_specs=[anywhere] + [loca...]
    pallas_call x1, Pallas kernels: 83.4 us -> 80 us  [finish(): pl.pallas_call(functools.partial(finish_kernel, fused), out_shape=outs, i...]
where the time goes in v2:
time: 109 us; the launch traced here: 108 us
  Pallas kernels  107 us (98%)
    pallas_call x1, Pallas kernels, finish(): pl.pallas_call(functools.partial(finish_kernel, fused), out_shape=outs, i...  80 us
    pallas_call x1, Pallas kernels, attend(): pl.pallas_call(attend_kernel, out_shape=outs, in_specs=[anywhere] + [loca...  24.2 us
    pallas_call x1, Pallas kernels, deliver(): pl.pallas_call(functools.partial(deliver_kernel, len(arrays)), out_shape=...  3.11 us

profile of v2, /device:TPU:1, one launch (start us, length us, event | category | flops | bytes accessed | tf_op | source)
XLA Modules:
  0.0 108.2 jit_solution(15940458893231880480)
XLA Ops:
  0.6 24.2 %attend.1 = (bf16[1024,768]{1,0:T(8,128)(2,1)}, bf16[3,1024,128]{2,1,0:T(8,128)(2,1)}, bf16[3,1024,128]{2,1,0:T(8,128)(2,1)}, bf16[3,1024,128]{2,1,0:T(8,128)(2,...) custom-call(bf16[512,768]{1,0:T(8,128)(2,1)} %bitcast.4, ...), custom_call_target="tpu_custom_call" | custom-call | tf_op jit(solution)/shard_map/attend/pallas_call | solution.py:338
  24.9 80.0 %finish.1 = (bf16[512,768]{1,0:T(8,128)(2,1)}, bf16[512,768]{1,0:T(8,128)(2,1)}, bf16[1,2,192,384]{3,2,1,0:T(8,128)(2,1)}, bf16[2,2,48,768]{3,2,1,0:T(8,128)(2,1...) custom-call(bf16[512,768]{1,0:T(8,128)(2,1)} %bitcast.5, ...), custom_call_target="tpu_custom_call" | custom-call | tf_op jit(solution)/shard_map/finish/pallas_call | solution.py:1369
  104.9 3.1 %deliver.1 = (bf16[512,768]{1,0:T(8,128)(2,1)}, bf16[512,768]{1,0:T(8,128)(2,1)}, f32[1,512]{1,0:T(1,128)}, f32[48,768]{1,0:T(8,128)}, f32[48,768]{1,0:T(8,128)}...) custom-call(bf16[512,768]{1,0:T(8,128)(2,1)} %get-tuple-element.60.r, ...), custom_call_target="tpu_custom_call" | custom-call | tf_op jit(solution)/shard_map/deliver/pallas_call | solution.py:1458

commit v3 on v2

--- a/solution.py
+++ b/solution.py
@@ -58,294 +58,6 @@
 def rows_of(start, size):
     return pl.ds(pl.multiple_of(start, size), size)
 
-
-def attend_kernel(
-    tokens,
-    seg,
-    gain,
-    shift,
-    w_query,
-    w_key,
-    w_value,
-    low_in_out,
-    query_out,
-    key_out,
-    value_out,
-    prob_outs,
-    slopes_out,
-    heads_out,
-    other_out,
-    scales_out,
-    share_out,
-    all_tokens,
-    low_in,
-    weights,
-    queries,
-    keys,
-    values,
-    lead_query,
-    lead_key,
-    probs,
-    slopes,
-    penalty,
-    heads,
-    scales,
-    scale_cols,
-    seg_cols,
-    free_cols,
-    running,
-    numerator,
-    pairs_seen,
-    far_send,
-    far_recv,
-    head_send,
-    head_recv,
-    weight_sems,
-    out_sems,
-    prob_sems,
-):
-    core = lax.axis_index("keys")
-    row = lax.axis_index("rows")
-    other = 1 - core
-    partner = (row, other)
-    half, width = tokens.shape
-    length = 2 * half
-    mine = width // 2
-    pair_count = mine // PAIR
-    tiles = length // TILE
-
-    columns = pl.ds(pl.multiple_of(core * mine, 128), mine)
-    loads = []
-    for place, source in enumerate((w_query, w_key, w_value)):
-        loads.append((source.at[:, columns], weights.at[:, pl.ds(place * mine, mine)]))
-    for place, source in enumerate((w_query, w_key)):
-        loads.append(
-            (source.at[:, pl.ds(0, PAIR)], weights.at[:, pl.ds(3 * mine + place * PAIR, PAIR)])
-        )
-    own = rows_of(core * half, half)
-    loads = [
-        pltpu.make_async_copy(source, target, weight_sems.at[i])
-        for i, (source, target) in enumerate(loads)
-    ]
-    own_load = pltpu.make_async_copy(tokens, all_tokens.at[own], weight_sems.at[5])
-    own_load.start()
-    for one in loads:
-        one.start()
-
-    barrier = pltpu.get_barrier_semaphore()
-    pl.semaphore_signal(barrier, inc=1, device_id=partner, device_id_type=MESH)
-    pl.semaphore_wait(barrier, 1)
-    exchange = remote(tokens, all_tokens.at[own], far_send, far_recv, partner)
-    exchange.start()
-
-    seg_row = seg[...]
-    seg_wide = jnp.broadcast_to(seg_row.astype(FULL), (128, length))
-    spot = lax.broadcasted_iota(jnp.int32, (128, length), 1)
-    before = pltpu.roll(seg_wide, 1, 1)
-    free_wide = jnp.where((spot > 0) & (before == seg_wide), 1.0, 0.0)
-    seg_cols[...] = seg_wide.T
-    free_cols[...] = free_wide.T
-    own_load.wait()
-
-    keep = lanes_below((TILE, PAIR), HEAD)
-
-    @pl.loop(0, tiles)
-    def _(i):
-        @pl.when(i == half // TILE)
-        def _():
-            exchange.wait_recv()
-
-        here = rows_of(lax.rem(core * (half // TILE) + i, tiles) * TILE, TILE)
-        unit, _ = layer_norm(all_tokens[here, :].astype(FULL))
-        low_in[here, :] = (unit * flat(gain) + flat(shift)).astype(LOW)
-
-        @pl.when(i == 0)
-        def _():
-            for one in loads:
-                one.wait()
-
-        result = contract(low_in[here, :], weights[...], 1, 0).astype(LOW)
-        for p in range(pair_count):
-            queries[p, here, :] = result[:, p * PAIR : (p + 1) * PAIR] * LOW(0.125)
-            keys[p, here, :] = result[:, mine + p * PAIR : mine + (p + 1) * PAIR]
-            values[p, here, :] = result[:, 2 * mine + p * PAIR : 2 * mine + (p + 1) * PAIR]
-        first = result[:, 3 * mine : 3 * mine + PAIR]
-        lead_query[here, :] = jnp.where(keep, first, LOW(0.0)) * LOW(0.125)
-        lead_key[here, :] = result[:, 3 * mine + PAIR :]
-
-    puts = [
-        pltpu.make_async_copy(low_in, low_in_out, out_sems.at[0]),
-        pltpu.make_async_copy(queries, query_out, out_sems.at[1]),
-        pltpu.make_async_copy(keys, key_out, out_sems.at[2]),
-        pltpu.make_async_copy(values, value_out, out_sems.at[3]),
-    ]
-    for one in puts:
-        one.start()
-
-    spots = (
-        lax.broadcasted_iota(jnp.int32, (2 * TILE, 2 * TILE), 0),
-        lax.broadcasted_iota(jnp.int32, (2 * TILE, 2 * TILE), 1),
-    )
-    earlier = jnp.where(spots[0] < spots[1], 1.0, 0.0).astype(LOW)
-    scales[...] = jnp.zeros_like(scales)
-    running[...] = jnp.zeros_like(running)
-    numerator[...] = jnp.zeros_like(numerator)
-    pairs_seen[...] = jnp.zeros_like(pairs_seen)
-
-    @pl.loop(0, (tiles // 2) * (tiles // 2 + 1) // 2)
-    def _(step):
-        wide, k = corner(step, tiles // 2)
-        rows, span = rows_of(k * 2 * TILE, 2 * TILE), rows_of(wide * 2 * TILE, 2 * TILE)
-        scores = contract(lead_key[rows, :], lead_query[span, :], 1, 1)
-        repeat = 2 * TILE // 128
-        same = jnp.concatenate([seg_cols[rows, :]] * repeat, 1) == seg[:, span].astype(FULL)
-        ahead = spots[1] - spots[0] + (wide - k) * 2 * TILE
-        later = same & (ahead > 0)
-        allowed = same & (ahead >= 0)
-        select = jnp.where(later, jnp.concatenate([free_cols[rows, :]] * repeat, 1), 0.0)
-        level = scores - SELECT_SHIFT
-        chosen = select * (jnp.maximum(level, 0.0) + jnp.log(1.0 + jnp.exp(-jnp.abs(level))))
-        slope = (select * (0.5 + 0.5 * jnp.tanh(0.5 * level))).astype(LOW)
-
-        slopes[wide * (2 * wide + 1) + 2 * k] = slope[:TILE, :TILE]
-
-        @pl.when(k < wide)
-        def _():
-            slopes[wide * (2 * wide + 1) + 2 * k + 1] = slope[TILE:, :TILE]
-
-        slopes[(2 * wide + 1) * (wide + 1) + 2 * k] = slope[:TILE, TILE:]
-        slopes[(2 * wide + 1) * (wide + 1) + 2 * k + 1] = slope[TILE:, TILE:]
-        high = chosen.astype(LOW)
-        rest = (chosen - high.astype(FULL)).astype(LOW)
-        total = (
-            running[rows, :] + contract(high, earlier, 1, 0) + contract(rest, earlier, 1, 0)
-        )
-        penalty[rows, span] = jnp.where(allowed, total, MASKED)
-        running[rows, :] += jnp.sum(chosen, -1, keepdims=True)
-        share = jnp.where(later, 0.5 + 0.5 * jnp.tanh(0.5 * total - 1.0), 0.0)
-        numerator[rows, :] += jnp.sum(share, -1, keepdims=True)
-        pairs_seen[rows, :] += jnp.sum(jnp.where(later, 1.0, 0.0), -1, keepdims=True)
-
-    slope_put = pltpu.make_async_copy(slopes, slopes_out, out_sems.at[4])
-    slope_put.start()
-
-    shares = numerator[own, :] / jnp.maximum(pairs_seen[own, :], 1.0)
-    share_out[...] = jnp.broadcast_to(shares, (half, 128)).T[0:8, :]
-
-    def put_probs(p, t):
-        return pltpu.make_async_copy(
-            probs[t].at[p], prob_outs[t].at[p], prob_sems.at[p, t]
-        )
-
-    def send_heads(p):
-        return remote(
-            heads.at[p, rows_of(other * half, half)],
-            other_out.at[p],
-            head_send.at[p],
-            head_recv.at[p],
-            partner,
-        )
-
-    @pl.loop(0, pair_count)
-    def _(p):
-        for t in range(tiles):
-            count = (t + 1) * TILE
-            span = pl.ds(t * TILE, TILE)
-            query = queries[p, span, :]
-            both = jnp.concatenate(
-                [jnp.where(keep, query, LOW(0.0)), jnp.where(keep, LOW(0.0), query)], 0
-            )
-            fine = penalty[pl.ds(0, count), span]
-            logits = contract(keys[p, pl.ds(0, count), :], both, 1, 1) - jnp.concatenate(
-                [fine, fine], 1
-            )
-            scaled = jnp.exp(logits - jnp.max(logits, 0, keepdims=True))
-            prob = scaled.astype(LOW)
-            probs[t][p] = prob
-            scale = 1.0 / jnp.sum(scaled, 0, keepdims=True)
-            scales[pl.ds(2 * p, 1), span] = scale[:, :TILE]
-            scales[pl.ds(2 * p + 1, 1), span] = scale[:, TILE:]
-            out = contract(values[p, pl.ds(0, count), :], prob, 0, 0) * scale
-            out = jnp.concatenate([out[:HEAD, :TILE], out[HEAD:, TILE:]], 0)
-            heads[p, span, :] = out.T.astype(LOW)
-        for t in range(tiles):
-            put_probs(p, t).start()
-        send_heads(p).start()
-
-    scale_cols[...] = scales[...].T
-    scale_put = pltpu.make_async_copy(scale_cols, scales_out, out_sems.at[6])
-    scale_put.start()
-    last = pltpu.make_async_copy(heads, heads_out, out_sems.at[5])
-    last.start()
-    for p in range(pair_count):
-        send_heads(p).wait()
-        for t in range(tiles):
-            put_probs(p, t).wait()
-    for one in puts + [slope_put, scale_put, last]:
-        one.wait()
-    exchange.wait_send()
-
-
-def attend(tokens, seg, gain, shift, w_query, w_key, w_value):
-    half, width = tokens.shape
-    length, mine = 2 * half, width // 2
-    pairs, tiles = mine // PAIR, 2 * half // TILE
-    spans = [(t + 1) * TILE for t in range(tiles)]
-    corners = tiles * (tiles + 1) // 2
-    outs = [
-        jax.ShapeDtypeStruct((length, width), LOW),
-        jax.ShapeDtypeStruct((pairs, length, PAIR), LOW),
-        jax.ShapeDtypeStruct((pairs, length, PAIR), LOW),
-        jax.ShapeDtypeStruct((pairs, length, PAIR), LOW),
-        [jax.ShapeDtypeStruct((pairs, span, 2 * TILE), LOW) for span in spans],
-        jax.ShapeDtypeStruct((corners, TILE, TILE), LOW),
-        jax.ShapeDtypeStruct((pairs, length, PAIR), LOW),
-        jax.ShapeDtypeStruct((pairs, half, PAIR), LOW),
-        jax.ShapeDtypeStruct((length, 128), FULL),
-        jax.ShapeDtypeStruct((8, half), FULL),
-    ]
-    anywhere = pl.BlockSpec(memory_space=pl.ANY)
-    local = pl.BlockSpec(memory_space=pltpu.VMEM)
-    out_specs = [anywhere] * 4 + [[anywhere] * tiles, anywhere, anywhere, anywhere, anywhere, local]
-    scratch = [
-        pltpu.VMEM((length, width), LOW),
-        pltpu.VMEM((length, width), LOW),
-        pltpu.VMEM((width, 3 * mine + 2 * PAIR), LOW),
-        pltpu.VMEM((pairs, length, PAIR), LOW),
-        pltpu.VMEM((pairs, length, PAIR), LOW),
-        pltpu.VMEM((pairs, length, PAIR), LOW),
-        pltpu.VMEM((length, PAIR), LOW),
-        pltpu.VMEM((length, PAIR), LOW),
-        [pltpu.VMEM((pairs, span, 2 * TILE), LOW) for span in spans],
-        pltpu.VMEM((corners, TILE, TILE), LOW),
-        pltpu.VMEM((length, length), FULL),
-        pltpu.VMEM((pairs, length, PAIR), LOW),
-        pltpu.VMEM((128, length), FULL),
-        pltpu.VMEM((length, 128), FULL),
-        pltpu.VMEM((length, 128), FULL),
-        pltpu.VMEM((length, 128), FULL),
-        pltpu.VMEM((length, 1), FULL),
-        pltpu.VMEM((length, 1), FULL),
-        pltpu.VMEM((length, 1), FULL),
-        pltpu.SemaphoreType.DMA,
-        pltpu.SemaphoreType.DMA,
-        pltpu.SemaphoreType.DMA((pairs,)),
-        pltpu.SemaphoreType.DMA((pairs,)),
-        pltpu.SemaphoreType.DMA((6,)),
-        pltpu.SemaphoreType.DMA((7,)),
-        pltpu.SemaphoreType.DMA((pairs, tiles)),
-    ]
-    return pl.pallas_call(
-        attend_kernel,
-        out_shape=outs,
-        in_specs=[anywhere] + [local] * 3 + [anywhere] * 3,
-        out_specs=out_specs,
-        scratch_shapes=scratch,
-        compiler_params=pltpu.CompilerParams(
-            collective_id=1, has_side_effects=True, vmem_limit_bytes=VMEM_LIMIT
-        ),
-        name="attend",
-    )(tokens, seg, gain, shift, w_query, w_key, w_value)
 
 def gelu_parts(field):
     scale = 0.7978845608028654
@@ -378,7 +90,7 @@
     }
 
 
-def finish_kernel(fused, *refs):
+def layer_kernel(fused, *refs):
     refs = list(refs)
 
     def take(count):
@@ -386,13 +98,11 @@
         del refs[:count]
         return taken if count > 1 else taken[0]
 
-    tokens, cotangent, gain_in, gain_mid, shift_mid = take(5)
-    low_in_hbm, query_hbm, key_hbm, value_hbm = take(4)
-    prob_hbm, slope_hbm = take(4), take(1)
-    heads_hbm, other_hbm, scales_hbm = take(3)
+    tokens_hbm, seg, cotangent, gain, shift, gain_mid, shift_mid = take(7)
     w_query, w_key, w_value, w_out, w_up, w_down = take(6)
     output, input_grad = take(2)
     results = dict(zip(KINDS, take(len(KINDS))))
+    prob_hbm, slope_hbm, share_out = take(4), take(1), take(1)
     (
         grads_all,
         weight_out,
@@ -408,12 +118,13 @@
         keys,
         values,
         scales,
-    ) = take(14)
+        tokens,
+    ) = take(15)
     probs = take(4)
-    share_send, share_recv = take(2)
-    stage, stage_far, catch_mid, catch_out = take(4)
+    share = take(1)
+    stage, catch_mid, catch_out = take(3)
     weight_down, hidden_low = take(2)
-    stage_down, stage_out = take(2)
+    stage_out = take(1)
     vec_sums = take(1)
     parts = dict(zip(KINDS, take(len(KINDS))))
     if fused:
@@ -430,6 +141,7 @@
         for kind in KINDS:
             sems[kind + "5"] = take(1)
     (load_sems, g_sems, mid_sems, dz_sems, a_sems, b_sems, c_sems, pd_sems, po_sems, df_sems, prob_sems) = take(11)
+    far_sems, head_sems, weight_sems = take(3)
 
     long, wide, deep = GRID
     core = lax.axis_index("keys")
@@ -712,20 +424,14 @@
     out_put = local(low_mid.at[pl.ds(half, half)], output, 1)
     g_load = local(cotangent, grads_all.at[own], 0)
     out_loads = [
+        local(tokens_hbm, tokens, 15),
         local(w_out.at[rows_of(core * mine, mine)], weight_out.at[pl.ds(0, mine)], 1),
         local(w_out.at[rows_of(other * mine, mine)], weight_out.at[pl.ds(mine, mine)], 2),
-        local(heads_hbm, heads, 3),
-        local(other_hbm, heads_far, 4),
     ]
-    late_loads = [
-        local(low_in_hbm, low_in, 5),
-        local(query_hbm, queries, 6),
-        local(key_hbm, keys, 7),
-        local(value_hbm, values, 8),
-        local(scales_hbm, scales, 14),
+    down_loads = [
+        local(w_down.at[rows_of((core * 2 + b) * block, block)], weight_down.at[b], 11 + b)
+        for b in range(2)
     ]
-    for one in out_loads:
-        one.start()
 
     peers = [partner]
     if fused:
@@ -735,6 +441,23 @@
     for peer in peers:
         pl.semaphore_signal(barrier, inc=1, device_id=peer, device_id_type=MESH)
 
+    exchange = remote(tokens_hbm, low_resid.at[own], far_sems.at[0], far_sems.at[1], partner)
+
+    def send_heads(p):
+        return remote(
+            heads.at[p, rows_of(far_start, half)],
+            heads_far.at[p],
+            head_sems.at[0, p],
+            head_sems.at[1, p],
+            partner,
+        )
+
+    def prob_put(t):
+        return pltpu.make_async_copy(probs[t].at[0], prob_hbm[t], prob_sems.at[t, 0])
+
+    def prob_load(t):
+        return pltpu.make_async_copy(prob_hbm[t], probs[t].at[0], prob_sems.at[t, 1])
+
     def own_rows(i):
         return rows_of(own_start + i * TILE, TILE)
 
@@ -766,10 +489,180 @@
         lambda i: stage.at[tile_rows(i)], lambda i: catch_mid.at[tile_rows(i)], b_sems
     )
     out_back = to_partner(
-        lambda i: stage_far.at[tile_rows(i)], lambda i: catch_out.at[tile_rows(i)], c_sems
-    )
-
-    def feed_forward(weight_up, grad_up):
+        lambda i: stage.at[tile_rows(i)], lambda i: catch_out.at[tile_rows(i)], c_sems
+    )
+
+    def forward(
+        weights,
+        lead_query,
+        lead_key,
+        slopes,
+        penalty,
+        scale_rows,
+        seg_cols,
+        free_cols,
+        sums,
+    ):
+        def column(rows, i):
+            return (rows, pl.ds(i, 1))
+
+        columns = pl.ds(pl.multiple_of(core * mine, 128), mine)
+        loads = []
+        for place, source in enumerate((w_query, w_key, w_value)):
+            loads.append((source.at[:, columns], weights.at[:, pl.ds(place * mine, mine)]))
+        for place, source in enumerate((w_query, w_key)):
+            loads.append(
+                (source.at[:, pl.ds(0, PAIR)], weights.at[:, pl.ds(3 * mine + place * PAIR, PAIR)])
+            )
+        loads = [
+            pltpu.make_async_copy(source, target, weight_sems.at[i])
+            for i, (source, target) in enumerate(loads)
+        ]
+        own_load = pltpu.make_async_copy(tokens_hbm, low_resid.at[own], weight_sems.at[5])
+        own_load.start()
+        for one in loads:
+            one.start()
+
+        pl.semaphore_wait(barrier, len(peers))
+        exchange.start()
+        g_far.start()
+        for one in out_loads + [g_load] + down_loads:
+            one.start()
+
+        own_load.wait()
+
+        keep = lanes_below((TILE, PAIR), HEAD)
+        keep_half = lanes_below((half, PAIR), HEAD)
+
+        @pl.loop(0, 2)
+        def _(i):
+            @pl.when(i == 1)
+            def _():
+                exchange.wait_recv()
+
+            here = rows_of(lax.rem(core + i, 2) * half, half)
+            unit, _ = layer_norm(low_resid[here, :].astype(FULL))
+            low_in[here, :] = (unit * flat(gain) + flat(shift)).astype(LOW)
+
+            @pl.when(i == 0)
+            def _():
+                seg_row = seg[...]
+                seg_wide = jnp.broadcast_to(seg_row.astype(FULL), (128, length))
+                spot = lax.broadcasted_iota(jnp.int32, (128, length), 1)
+                before = pltpu.roll(seg_wide, 1, 1)
+                free_wide = jnp.where((spot > 0) & (before == seg_wide), 1.0, 0.0)
+                seg_cols[...] = seg_wide.T
+                free_cols[...] = free_wide.T
+                for one in loads:
+                    one.wait()
+
+            result = contract(low_in[here, :], weights[...], 1, 0).astype(LOW)
+            for p in range(pair_count):
+                queries[p, here, :] = result[:, p * PAIR : (p + 1) * PAIR] * LOW(0.125)
+                keys[p, here, :] = result[:, mine + p * PAIR : mine + (p + 1) * PAIR]
+                values[p, here, :] = result[:, 2 * mine + p * PAIR : 2 * mine + (p + 1) * PAIR]
+            first = result[:, 3 * mine : 3 * mine + PAIR]
+            lead_query[here, :] = jnp.where(keep_half, first, LOW(0.0)) * LOW(0.125)
+            lead_key[here, :] = result[:, 3 * mine + PAIR :]
+
+        spots = (
+            lax.broadcasted_iota(jnp.int32, (2 * TILE, 2 * TILE), 0),
+            lax.broadcasted_iota(jnp.int32, (2 * TILE, 2 * TILE), 1),
+        )
+        earlier = jnp.where(spots[0] < spots[1], 1.0, 0.0).astype(LOW)
+        scale_rows[...] = jnp.zeros_like(scale_rows)
+        sums[...] = jnp.zeros_like(sums)
+
+        @pl.loop(0, (tiles // 2) * (tiles // 2 + 1) // 2)
+        def _(step):
+            wide, k = corner(step, tiles // 2)
+            rows, span = rows_of(k * 2 * TILE, 2 * TILE), rows_of(wide * 2 * TILE, 2 * TILE)
+            scores = contract(lead_key[rows, :], lead_query[span, :], 1, 1)
+            repeat = 2 * TILE // 128
+            same = jnp.concatenate([seg_cols[rows, :]] * repeat, 1) == seg[:, span].astype(FULL)
+            ahead = spots[1] - spots[0] + (wide - k) * 2 * TILE
+            later = same & (ahead > 0)
+            allowed = same & (ahead >= 0)
+            select = jnp.where(later, jnp.concatenate([free_cols[rows, :]] * repeat, 1), 0.0)
+            level = scores - SELECT_SHIFT
+            chosen = select * (jnp.maximum(level, 0.0) + jnp.log(1.0 + jnp.exp(-jnp.abs(level))))
+            slope = (select * (0.5 + 0.5 * jnp.tanh(0.5 * level))).astype(LOW)
+
+            slopes[wide * (2 * wide + 1) + 2 * k] = slope[:TILE, :TILE]
+
+            @pl.when(k < wide)
+            def _():
+                slopes[wide * (2 * wide + 1) + 2 * k + 1] = slope[TILE:, :TILE]
+
+            slopes[(2 * wide + 1) * (wide + 1) + 2 * k] = slope[:TILE, TILE:]
+            slopes[(2 * wide + 1) * (wide + 1) + 2 * k + 1] = slope[TILE:, TILE:]
+            high = chosen.astype(LOW)
+            rest = (chosen - high.astype(FULL)).astype(LOW)
+            total = (
+                sums[column(rows, 0)] + contract(high, earlier, 1, 0) + contract(rest, earlier, 1, 0)
+            )
+            penalty[rows, span] = jnp.where(allowed, total, MASKED)
+            sums[column(rows, 0)] += jnp.sum(chosen, -1, keepdims=True)
+            ratio = jnp.where(later, 0.5 + 0.5 * jnp.tanh(0.5 * total - 1.0), 0.0)
+            sums[column(rows, 1)] += jnp.sum(ratio, -1, keepdims=True)
+            sums[column(rows, 2)] += jnp.sum(jnp.where(later, 1.0, 0.0), -1, keepdims=True)
+
+        slope_put = pltpu.make_async_copy(slopes, slope_hbm, weight_sems.at[6])
+        slope_put.start()
+
+        shares = sums[column(own, 1)] / jnp.maximum(sums[column(own, 2)], 1.0)
+        share_out[...] = jnp.broadcast_to(shares, (half, 128)).T[0:8, :]
+
+        @pl.loop(0, pair_count)
+        def _(p):
+            slot = lax.rem(p, 2)
+
+            @pl.when(p == 2)
+            def _():
+                for t in range(tiles):
+                    prob_put(t).wait()
+
+            for t in range(tiles):
+                count = (t + 1) * TILE
+                span = pl.ds(t * TILE, TILE)
+                query = queries[p, span, :]
+                both = jnp.concatenate(
+                    [jnp.where(keep, query, LOW(0.0)), jnp.where(keep, LOW(0.0), query)], 0
+                )
+                fine = penalty[pl.ds(0, count), span]
+                logits = contract(keys[p, pl.ds(0, count), :], both, 1, 1) - jnp.concatenate(
+                    [fine, fine], 1
+                )
+                scaled = jnp.exp(logits - jnp.max(logits, 0, keepdims=True))
+                prob = scaled.astype(LOW)
+                probs[t][slot] = prob
+                scale = 1.0 / jnp.sum(scaled, 0, keepdims=True)
+                scale_rows[pl.ds(2 * p, 1), span] = scale[:, :TILE]
+                scale_rows[pl.ds(2 * p + 1, 1), span] = scale[:, TILE:]
+                out = contract(values[p, pl.ds(0, count), :], prob, 0, 0) * scale
+                out = jnp.concatenate([out[:HEAD, :TILE], out[HEAD:, TILE:]], 0)
+                heads[p, span, :] = out.T.astype(LOW)
+            @pl.when(p == 0)
+            def _():
+                for t in range(tiles):
+                    prob_put(t).start()
+
+            send_heads(p).start()
+
+        scales[...] = scale_rows[...].T
+        slope_put.wait()
+        exchange.wait_send()
+
+    def feed_forward(weight_up, grad_up, stage_down):
+        def give_down(b):
+            return remote(
+                stage_down.at[b],
+                parts["down"].at[0, core * 2 + b],
+                pd_sems.at[0, b],
+                pd_sems.at[1, b],
+                partner,
+            )
+
         up_loads = [
             local(
                 w_up.at[:, pl.ds(pl.multiple_of((core * 2 + b) * block, 128), block)],
@@ -778,14 +671,12 @@
             )
             for b in range(2)
         ]
-        down_loads = [
-            local(w_down.at[rows_of((core * 2 + b) * block, block)], weight_down.at[b], 11 + b)
-            for b in range(2)
-        ]
+        for one in up_loads:
+            one.start()
         for one in out_loads:
             one.wait()
-        for one in up_loads + [g_load] + down_loads:
-            one.start()
+        for p in range(pair_count):
+            send_heads(p).wait_recv()
 
         @pl.loop(0, 2)
         def _(i):
@@ -800,18 +691,11 @@
             unit, _ = layer_norm(field)
             low_mid[place, :] = (unit * flat(gain_mid) + flat(shift_mid)).astype(LOW)
 
-            @pl.when(i == 0)
-            def _():
-                pl.semaphore_wait(barrier, len(peers))
-
             mid_far(i).start()
 
-        g_far.start()
 
         for one in up_loads:
             one.wait()
-        for one in late_loads:
-            one.start()
 
         @pl.loop(0, 2)
         def _(b):
@@ -926,17 +810,9 @@
 
         for i in range(2):
             mid_back(i).wait_send()
+            give_down(i).wait_send()
         if fused:
             down.turn_at(core * 2 + 1)
-
-    def give_down(b):
-        return remote(
-            stage_down.at[b],
-            parts["down"].at[0, core * 2 + b],
-            pd_sems.at[0, b],
-            pd_sems.at[1, b],
-            partner,
-        )
 
     give_out = remote(
         stage_out,
@@ -948,17 +824,25 @@
 
     vec_sums[...] = jnp.zeros_like(vec_sums)
     pl.run_scoped(
+        forward,
+        pltpu.VMEM((width, 3 * mine + 2 * PAIR), LOW),
+        pltpu.VMEM((length, PAIR), LOW),
+        pltpu.VMEM((length, PAIR), LOW),
+        pltpu.VMEM((tiles * (tiles + 1) // 2, TILE, TILE), LOW),
+        pltpu.VMEM((length, length), FULL),
+        pltpu.VMEM((128, length), FULL),
+        pltpu.VMEM((length, 128), FULL),
+        pltpu.VMEM((length, 128), FULL),
+        pltpu.VMEM((length, 128), FULL),
+    )
+    pl.run_scoped(
         feed_forward,
         pltpu.VMEM((2, width, block), LOW),
         pltpu.VMEM((2, length, block), LOW),
-    )
-
-    def prob_load(p, t, slot):
-        return pltpu.make_async_copy(prob_hbm[t].at[p], probs[t].at[slot], prob_sems.at[t, slot])
+        pltpu.VMEM((2, wide, deep) + block_shapes(width, hidden)["down"][0], LOW),
+    )
 
     def attention(slopes, fades, key_sum, value_sum, carry, grad_qkv, weight_in):
-        for t in range(tiles):
-            prob_load(pair_count - 1, t, 0).start()
         slope_load = local(slope_hbm, slopes, 13)
         weight_loads = []
         for place, source in enumerate((w_query, w_key, w_value)):
@@ -974,9 +858,6 @@
             one.start()
 
         keep = lanes_below((TILE, PAIR), HEAD)
-        for one in late_loads:
-            one.wait()
-
         def head_grads(here):
             result = contract(low_resid[here, :], weight_out[pl.ds(0, mine), :], 1, 1)
             for p in range(pair_count):
@@ -1017,8 +898,8 @@
         def fade_send(t):
             part = pl.ds(t * (t + 1) // 2, t + 1)
             return remote(
-                share_send.at[part],
-                share_recv.at[part],
+                share.at[part],
+                share.at[part],
                 df_sems.at[0, t],
                 df_sems.at[1, t],
                 partner,
@@ -1026,13 +907,15 @@
 
         def pair_step(step, p):
             slot = lax.rem(step, 2)
-            for t in range(tiles):
-                prob_load(p, t, slot).wait()
-
-            @pl.when(step < pair_count - 1)
+            @pl.when(step == 1)
             def _():
                 for t in range(tiles):
-                    prob_load(p - 1, t, 1 - slot).start()
+                    prob_load(t).start()
+
+            @pl.when(step == 2)
+            def _():
+                for t in range(tiles):
+                    prob_load(t).wait()
 
             for t in reversed(range(tiles)):
                 count = (t + 1) * TILE
@@ -1075,6 +958,11 @@
                 grad_qkv[p, span, pl.ds(0, PAIR)] = (query_part.T * 0.125).astype(LOW)
 
                 if t == tiles - 1:
+                    @pl.when(step == 0)
+                    def _():
+                        give_out.wait_recv()
+                        steps("out start")
+
                     steps_when(step == 1, "up1 turn")
                     steps_when(step == 2, "attn2 turn", "up1 gather")
 
@@ -1087,7 +975,7 @@
                     span, rows = pl.ds(t * TILE, TILE), pl.ds(0, count)
                     part = pl.ds(t * (t + 1) // 2, t + 1)
                     fade_send(t).wait_recv()
-                    total = fades[rows, span] + share_recv[part].astype(FULL).reshape(count, TILE)
+                    total = fades[rows, span] + share[part].astype(FULL).reshape(count, TILE)
                     later = contract(total.astype(LOW), after, 1, 0) + carry[rows, :]
                     if t:
                         carry[rows, :] += jnp.sum(total, -1, keepdims=True)
@@ -1129,17 +1017,14 @@
                 grad_qkv[p, :, pl.ds(PAIR, PAIR)] = key_sum[...].astype(LOW)
                 weights_into("attn", p - 1, grad_qkv[p])
 
-            @pl.when(step == 0)
-            def _():
-                give_out.wait_recv()
-                steps("out start", "up0 gather")
+            steps_when(step == 0, "up0 gather")
 
 
         @pl.when(core == 1)
         def _():
             for t in reversed(range(tiles)):
                 count = (t + 1) * TILE
-                share_send[pl.ds(t * (t + 1) // 2, t + 1)] = (
+                share[pl.ds(t * (t + 1) // 2, t + 1)] = (
                     fades[pl.ds(0, count), pl.ds(t * TILE, TILE)]
                     .astype(LOW)
                     .reshape(t + 1, TILE, TILE)
@@ -1204,7 +1089,7 @@
             unit, inverse = layer_norm(tokens[here, :].astype(FULL))
             vec_sums[0:1, :] += jnp.sum(grad * unit, 0, keepdims=True)
             vec_sums[1:2, :] += jnp.sum(grad, 0, keepdims=True)
-            scaled = grad * flat(gain_in)
+            scaled = grad * flat(gain)
             low_mid[here, :] = (
                 grad_resid[here, :]
                 + inverse
@@ -1258,15 +1143,15 @@
 
         @pl.when(i < 2)
         def _():
-            stage_far[tile_rows(i), :] = part.astype(LOW)
+            stage[tile_rows(i), :] = part.astype(LOW)
             out_back(i).start()
 
         @pl.when(i >= 2)
         def _():
             resid[tile_rows(i - 2), :] += part
 
-        steps_when(i == 0, "up1 close", "attn2 close")
-        steps_when(i == 1, "lead gather", "out close")
+        steps_when(i == 0, "lead gather", "up1 close", "attn2 close")
+        steps_when(i == 1, "out close")
         steps_when(i == 2, "vec gather")
         steps_when(i == 3, "attn1 close")
 
@@ -1291,13 +1176,13 @@
     g_far.wait_send()
     give_out.wait_send()
     for i in range(2):
-        give_down(i).wait_send()
         for one in (dz_far, out_back):
             one(i).wait_send()
-
-
-def finish(fused, tokens, cotangent, gain_in, gain_mid, shift_mid, forward, weights):
-    low_in, queries, keys, values, probs, slopes, heads, heads_far, scales = forward
+    for p in range(pair_count):
+        send_heads(p).wait_send()
+
+
+def layer(fused, tokens, seg, cotangent, gain_in, shift_in, gain_mid, shift_mid, weights):
     half, width = tokens.shape
     length, mine = 2 * half, width // 2
     hidden = weights[-1].shape[0]
@@ -1319,6 +1204,11 @@
         else:
             outs.append(jax.ShapeDtypeStruct((FAN[kind],) + GRID + shape, kept))
             out_specs.append(anywhere)
+    spans = [(t + 1) * TILE for t in range(tiles)]
+    outs += [jax.ShapeDtypeStruct((span, 2 * TILE), LOW) for span in spans]
+    outs.append(jax.ShapeDtypeStruct((tiles * (tiles + 1) // 2, TILE, TILE), LOW))
+    outs.append(jax.ShapeDtypeStruct((8, half), FULL))
+    out_specs += [anywhere] * (tiles + 1) + [local]
     scratch = [
         pltpu.VMEM((length, width), LOW),
         pltpu.VMEM((width, width), LOW),
@@ -1334,15 +1224,15 @@
         pltpu.VMEM((pairs, length, PAIR), LOW),
         pltpu.VMEM((pairs, length, PAIR), LOW),
         pltpu.VMEM((length, 128), FULL),
+        pltpu.VMEM((half, width), LOW),
     ]
     scratch += [pltpu.VMEM((2, (t + 1) * TILE, 2 * TILE), LOW) for t in range(tiles)]
     corners = tiles * (tiles + 1) // 2
-    scratch += [pltpu.VMEM((corners, TILE, TILE), LOW)] * 2
-    scratch += [pltpu.VMEM((half, width), LOW)] * 4
+    scratch += [pltpu.VMEM((corners, TILE, TILE), LOW)]
+    scratch += [pltpu.VMEM((half, width), LOW)] * 3
     block = hidden // 4
     scratch += [pltpu.VMEM((2, block, width), LOW), pltpu.VMEM((2, length, block), LOW)]
     scratch += [
-        pltpu.VMEM((2, wide, deep) + shapes["down"][0], LOW),
         pltpu.VMEM((2, wide, deep) + shapes["out"][0], LOW),
         pltpu.VMEM((8, width), FULL),
     ]
@@ -1366,33 +1256,19 @@
     scratch += [dma((17 + 3 * pairs,)), dma((2,))]
     scratch += [dma((2, 2))] * 6
     scratch += [dma((2,)), dma((2, tiles)), dma((tiles, 2))]
+    scratch += [dma((2,)), dma((2, pairs)), dma((7,))]
     return pl.pallas_call(
-        functools.partial(finish_kernel, fused),
+        functools.partial(layer_kernel, fused),
         out_shape=outs,
-        in_specs=[local] + [anywhere] + [local] * 3 + [anywhere] * (4 + tiles + 1 + 3 + 6),
+        in_specs=[anywhere, local, anywhere] + [local] * 4 + [anywhere] * 6,
         out_specs=out_specs,
         scratch_shapes=scratch,
         compiler_params=pltpu.CompilerParams(
             collective_id=0, has_side_effects=True, vmem_limit_bytes=VMEM_LIMIT
         ),
-        name="finish",
-    )(
-        tokens,
-        cotangent,
-        gain_in,
-        gain_mid,
-        shift_mid,
-        low_in,
-        queries,
-        keys,
-        values,
-        *probs,
-        slopes,
-        heads,
-        heads_far,
-        scales,
-        *weights,
-    )
+        name="layer",
+    )(tokens, seg, cotangent, gain_in, shift_in, gain_mid, shift_mid, *weights)
+
 
 def deliver_kernel(count, *refs):
     refs, (load_sems, put_sems) = refs[:-2], refs[-2:]
@@ -1522,19 +1398,18 @@
 ):
     fused = rows == COUNT
     own_tokens, own_grad = tokens[0], out_grad[0]
-    low_in, queries, keys, values, probs, slopes, heads, heads_far, scales, shares = attend(
-        own_tokens, seg_ids, gain_in, shift_in, w_query, w_key, w_value
-    )
-    output, input_grad, *parts = finish(
+    output, input_grad, *parts = layer(
         fused,
         own_tokens,
+        seg_ids,
         own_grad,
         gain_in,
+        shift_in,
         gain_mid,
         shift_mid,
-        (low_in, queries, keys, values, probs, slopes, heads, heads_far, scales),
         (w_query, w_key, w_value, w_out, w_up, w_down),
     )
+    parts, shares = parts[: len(KINDS)], parts[-1]
     if fused:
         output, input_grad, shares, *grads = deliver(output, input_grad, shares, *parts)
         grads, vectors = grads[:6], grads[6:]

time: 109 us -> 105 us (0.963)
  Pallas kernels: 107 us -> 103 us
    pallas_call x2 -> x1, Pallas kernels: 104 us -> 100 us  [layer(): pl.pallas_call(functools.partial(layer_kernel, fused), out_shape=outs, in...]
where the time goes in v3:
time: 105 us; the launch traced here: 104 us
  Pallas kernels  103 us (98%)
    pallas_call x1, Pallas kernels, layer(): pl.pallas_call(functools.partial(layer_kernel, fused), out_shape=outs, in...  100 us
    pallas_call x1, Pallas kernels, deliver(): pl.pallas_call(functools.partial(deliver_kernel, len(arrays)), out_shape=...  3.11 us

profile of v3, /device:TPU:1, one launch (start us, length us, event | category | flops | bytes accessed | tf_op | source)
XLA Modules:
  0.0 104.2 jit_solution(17624995210845907485)
XLA Ops:
  0.6 100.3 %layer.1 = (bf16[512,768]{1,0:T(8,128)(2,1)}, bf16[512,768]{1,0:T(8,128)(2,1)}, bf16[1,2,192,384]{3,2,1,0:T(8,128)(2,1)}, bf16[2,2,48,768]{3,2,1,0:T(8,128)(2,1)...) custom-call(bf16[512,768]{1,0:T(8,128)(2,1)} %bitcast.4, ...), custom_call_target="tpu_custom_call" | custom-call | tf_op jit(solution)/shard_map/layer/pallas_call | solution.py:1260
  101.0 3.1 %deliver.1 = (bf16[512,768]{1,0:T(8,128)(2,1)}, bf16[512,768]{1,0:T(8,128)(2,1)}, f32[1,512]{1,0:T(1,128)}, f32[48,768]{1,0:T(8,128)}, f32[48,768]{1,0:T(8,128)}...) custom-call(bf16[512,768]{1,0:T(8,128)(2,1)} %get-tuple-element.36.r, ...), custom_call_target="tpu_custom_call" | custom-call | tf_op jit(solution)/shard_map/deliver/pallas_call | solution.py:1334

commit v4 on v3

--- a/solution.py
+++ b/solution.py
@@ -112,19 +112,17 @@
         low_mid,
         grad_resid,
         low_resid,
-        grad_heads,
         low_in,
         queries,
         keys,
         values,
         scales,
         tokens,
-    ) = take(15)
+    ) = take(14)
     probs = take(4)
     share = take(1)
     stage, catch_mid, catch_out = take(3)
     weight_down, hidden_low = take(2)
-    stage_out = take(1)
     vec_sums = take(1)
     parts = dict(zip(KINDS, take(len(KINDS))))
     if fused:
@@ -285,13 +283,13 @@
                 one.wait()
 
     class Down(Job):
-        def near_copy(self, z):
+        def near_copy(self, z, s):
             send, recv = sems["down1"]
             return remote(
-                parts["down"].at[0, z, near],
-                got1["down"].at[0, z],
-                send.at[z],
-                recv.at[z],
+                parts["down"].at[0, z, near, s],
+                got1["down"].at[0, z, s],
+                send.at[z, s],
+                recv.at[z, s],
                 near_device,
             )
 
@@ -317,10 +315,21 @@
             )
 
         def start_at(self, z):
-            self.near_copy(z).start()
+            for s in range(deep):
+                self.near_copy(z, s).start()
+
+        def start_part(self, z, m):
+            @pl.when(core == 0)
+            def _():
+                self.near_copy(z, m).start()
+
+            @pl.when((core == 1) & (m == near))
+            def _():
+                self.start_at(z)
 
         def turn_at(self, z):
-            self.near_copy(z).wait_recv()
+            for s in range(deep):
+                self.near_copy(z, s).wait_recv()
 
             @pl.loop(0, deep)
             def _(b):
@@ -353,7 +362,8 @@
 
         def drain(self):
             for z in range(long):
-                self.near_copy(z).wait_send()
+                for s in range(deep):
+                    self.near_copy(z, s).wait_send()
             for step in range(1, long):
                 self.slow_copy(step).wait_send()
             self.next_copy().wait_send()
@@ -534,28 +544,13 @@
         keep = lanes_below((TILE, PAIR), HEAD)
         keep_half = lanes_below((half, PAIR), HEAD)
 
-        @pl.loop(0, 2)
-        def _(i):
-            @pl.when(i == 1)
-            def _():
-                exchange.wait_recv()
-
-            here = rows_of(lax.rem(core + i, 2) * half, half)
+        def normalize(whose):
+            here = rows_of(whose * half, half)
             unit, _ = layer_norm(low_resid[here, :].astype(FULL))
             low_in[here, :] = (unit * flat(gain) + flat(shift)).astype(LOW)
 
-            @pl.when(i == 0)
-            def _():
-                seg_row = seg[...]
-                seg_wide = jnp.broadcast_to(seg_row.astype(FULL), (128, length))
-                spot = lax.broadcasted_iota(jnp.int32, (128, length), 1)
-                before = pltpu.roll(seg_wide, 1, 1)
-                free_wide = jnp.where((spot > 0) & (before == seg_wide), 1.0, 0.0)
-                seg_cols[...] = seg_wide.T
-                free_cols[...] = free_wide.T
-                for one in loads:
-                    one.wait()
-
+        def project(whose):
+            here = rows_of(whose * half, half)
             result = contract(low_in[here, :], weights[...], 1, 0).astype(LOW)
             for p in range(pair_count):
                 queries[p, here, :] = result[:, p * PAIR : (p + 1) * PAIR] * LOW(0.125)
@@ -573,9 +568,7 @@
         scale_rows[...] = jnp.zeros_like(scale_rows)
         sums[...] = jnp.zeros_like(sums)
 
-        @pl.loop(0, (tiles // 2) * (tiles // 2 + 1) // 2)
-        def _(step):
-            wide, k = corner(step, tiles // 2)
+        def select_block(wide, k, diagonal=False):
             rows, span = rows_of(k * 2 * TILE, 2 * TILE), rows_of(wide * 2 * TILE, 2 * TILE)
             scores = contract(lead_key[rows, :], lead_query[span, :], 1, 1)
             repeat = 2 * TILE // 128
@@ -590,9 +583,11 @@
 
             slopes[wide * (2 * wide + 1) + 2 * k] = slope[:TILE, :TILE]
 
-            @pl.when(k < wide)
-            def _():
-                slopes[wide * (2 * wide + 1) + 2 * k + 1] = slope[TILE:, :TILE]
+            if not diagonal:
+
+                @pl.when(k < wide)
+                def _():
+                    slopes[wide * (2 * wide + 1) + 2 * k + 1] = slope[TILE:, :TILE]
 
             slopes[(2 * wide + 1) * (wide + 1) + 2 * k] = slope[:TILE, TILE:]
             slopes[(2 * wide + 1) * (wide + 1) + 2 * k + 1] = slope[TILE:, TILE:]
@@ -606,6 +601,26 @@
             ratio = jnp.where(later, 0.5 + 0.5 * jnp.tanh(0.5 * total - 1.0), 0.0)
             sums[column(rows, 1)] += jnp.sum(ratio, -1, keepdims=True)
             sums[column(rows, 2)] += jnp.sum(jnp.where(later, 1.0, 0.0), -1, keepdims=True)
+
+        normalize(core)
+        seg_row = seg[...]
+        seg_wide = jnp.broadcast_to(seg_row.astype(FULL), (128, length))
+        spot = lax.broadcasted_iota(jnp.int32, (128, length), 1)
+        before = pltpu.roll(seg_wide, 1, 1)
+        free_wide = jnp.where((spot > 0) & (before == seg_wide), 1.0, 0.0)
+        seg_cols[...] = seg_wide.T
+        free_cols[...] = free_wide.T
+        for one in loads:
+            one.wait()
+        project(core)
+        exchange.wait_recv()
+        select_block(core, core, True)
+        normalize(other)
+        project(other)
+
+        @pl.loop(0, 2)
+        def _(step):
+            select_block(other + step * core, other * (1 - step))
 
         slope_put = pltpu.make_async_copy(slopes, slope_hbm, weight_sems.at[6])
         slope_put.start()
@@ -724,7 +739,8 @@
             tall = hidden // COUNT
             per = mine // tall
             @pl.loop(0, 2)
-            def _(m):
+            def _(turn):
+                m = lax.rem(turn + core * near, 2)
                 place = pl.ds(pl.multiple_of(m * mine, 128), mine)
                 grad = contract(hidden_low[b, :, place], grads_all[...], 0, 0).astype(LOW)
                 kept = jnp.where(core == 0, grad[:, :mine], grad[:, mine:])
@@ -735,9 +751,10 @@
                     parts["down"][0, z, a, s] = kept[i * tall : (i + 1) * tall]
                     _, a, s = spot_of(rank, other)
                     stage_down[b, a, s] = given[i * tall : (i + 1) * tall]
+                if fused:
+                    down.start_part(core * 2 + b, m)
+
             give_down(b).start()
-            if fused:
-                down.start_at(core * 2 + b)
 
             @pl.loop(0, tiles)
             def _(i):
@@ -814,14 +831,6 @@
         if fused:
             down.turn_at(core * 2 + 1)
 
-    give_out = remote(
-        stage_out,
-        parts["out"].at[0, pl.ds(core * 2, 2)],
-        po_sems.at[0],
-        po_sems.at[1],
-        partner,
-    )
-
     vec_sums[...] = jnp.zeros_like(vec_sums)
     pl.run_scoped(
         forward,
@@ -842,7 +851,15 @@
         pltpu.VMEM((2, wide, deep) + block_shapes(width, hidden)["down"][0], LOW),
     )
 
-    def attention(slopes, fades, key_sum, value_sum, carry, grad_qkv, weight_in):
+    def attention(slopes, fades, key_sum, value_sum, carry, grad_qkv, weight_in, grad_heads, stage_out):
+        give_out = remote(
+            stage_out,
+            parts["out"].at[0, pl.ds(core * 2, 2)],
+            po_sems.at[0],
+            po_sems.at[1],
+            partner,
+        )
+
         slope_load = local(slope_hbm, slopes, 13)
         weight_loads = []
         for place, source in enumerate((w_query, w_key, w_value)):
@@ -1101,6 +1118,7 @@
             ).astype(LOW)
 
         in_put.start()
+        give_out.wait_send()
         for i in range(2):
             in_back(i).wait_send()
 
@@ -1113,6 +1131,8 @@
         pltpu.VMEM((length, 1), FULL),
         pltpu.VMEM((pair_count, length, mine), LOW),
         pltpu.VMEM((width, 3 * mine), LOW),
+        pltpu.VMEM((pair_count, length, PAIR), LOW),
+        pltpu.VMEM((2, wide, deep) + block_shapes(width, hidden)["out"][0], LOW),
     )
 
     if not fused:
@@ -1174,7 +1194,6 @@
     in_put.wait()
     out_put.wait()
     g_far.wait_send()
-    give_out.wait_send()
     for i in range(2):
         for one in (dz_far, out_back):
             one(i).wait_send()
@@ -1218,7 +1237,6 @@
         pltpu.VMEM((length, width), LOW),
         pltpu.VMEM((half, width), FULL),
         pltpu.VMEM((length, width), LOW),
-        pltpu.VMEM((pairs, length, PAIR), LOW),
         pltpu.VMEM((length, width), LOW),
         pltpu.VMEM((pairs, length, PAIR), LOW),
         pltpu.VMEM((pairs, length, PAIR), LOW),
@@ -1233,7 +1251,6 @@
     block = hidden // 4
     scratch += [pltpu.VMEM((2, block, width), LOW), pltpu.VMEM((2, length, block), LOW)]
     scratch += [
-        pltpu.VMEM((2, wide, deep) + shapes["out"][0], LOW),
         pltpu.VMEM((8, width), FULL),
     ]
     scratch += [pltpu.VMEM((FAN[kind],) + GRID + shapes[kind][0], shapes[kind][1]) for kind in KINDS]
@@ -1247,7 +1264,7 @@
                 pltpu.VMEM((FAN[kind],) + leads[kind][step] + shapes[kind][0], shapes[kind][1])
                 for kind in KINDS
             ]
-        scratch += [dma((long,))] * 2 + [dma((long - 1,))] * 2 + [dma((1,))] * 4
+        scratch += [dma((long, deep))] * 2 + [dma((long - 1,))] * 2 + [dma((1,))] * 4
         for kind in KINDS[1:]:
             fan = FAN[kind]
             count = 3 if kind == "vec" else fan
@@ -1279,12 +1296,15 @@
         pltpu.make_async_copy(source, target, load_sems.at[i])
         for i, (source, target) in enumerate(zip(sources, held))
     ]
-    for one in loads[2:] + loads[:2]:
+    for one in loads:
         one.start()
     puts = [
         pltpu.make_async_copy(source, target, put_sems.at[i])
         for i, (source, target) in enumerate(zip(held[:2] + made, targets))
     ]
+    for i in range(2):
+        loads[i].wait()
+        puts[i].start()
     for one in loads[2:]:
         one.wait()
     share_in, down, up, out, attn, early, lead, vec = held[2:]
@@ -1297,9 +1317,6 @@
     for k in range(2):
         g_down[:, k * mine : (k + 1) * mine] = down[0, k].astype(FULL)
     puts[8].start()
-    for i in range(2):
-        loads[i].wait()
-        puts[i].start()
     for k in range(2):
         start = k * mine
         g_out[:, start : start + mine] = out[0, k].astype(FULL)

time: 105 us -> 103 us (0.981)
    pallas_call x1, Pallas kernels: 100 us -> 98.9 us  [layer(): pl.pallas_call(functools.partial(layer_kernel, fused), out_shape=outs, in...]
where the time goes in v4:
time: 103 us
  Pallas kernels  102 us (99%)
    pallas_call x1, Pallas kernels, layer(): pl.pallas_call(functools.partial(layer_kernel, fused), out_shape=outs, in...  98.9 us
    pallas_call x1, Pallas kernels, deliver(): pl.pallas_call(functools.partial(deliver_kernel, len(arrays)), out_shape=...  3.07 us

profile of v4, /device:TPU:1, one launch (start us, length us, event | category | flops | bytes accessed | tf_op | source)
XLA Modules:
  0.0 102.8 jit_solution(7864867038613940885)
XLA Ops:
  0.6 98.9 %layer.1 = (bf16[512,768]{1,0:T(8,128)(2,1)}, bf16[512,768]{1,0:T(8,128)(2,1)}, bf16[1,2,192,384]{3,2,1,0:T(8,128)(2,1)}, bf16[2,2,48,768]{3,2,1,0:T(8,128)(2,1)...) custom-call(bf16[512,768]{1,0:T(8,128)(2,1)} %bitcast.4, ...), custom_call_target="tpu_custom_call" | custom-call | tf_op jit(solution)/shard_map/layer/pallas_call | solution.py:1277
  99.5 3.1 %deliver.1 = (bf16[512,768]{1,0:T(8,128)(2,1)}, bf16[512,768]{1,0:T(8,128)(2,1)}, f32[1,512]{1,0:T(1,128)}, f32[48,768]{1,0:T(8,128)}, f32[48,768]{1,0:T(8,128)}...) custom-call(bf16[512,768]{1,0:T(8,128)(2,1)} %get-tuple-element.36.r, ...), custom_call_target="tpu_custom_call" | custom-call | tf_op jit(solution)/shard_map/deliver/pallas_call | solution.py:1351

commit v5 on v4

--- a/solution.py
+++ b/solution.py
@@ -693,21 +693,17 @@
         for p in range(pair_count):
             send_heads(p).wait_recv()
 
-        @pl.loop(0, 2)
-        def _(i):
-            here, place = tile_rows(i), own_rows(i)
-            joined = jnp.concatenate(
-                [heads[p, place, :] for p in range(pair_count)]
-                + [heads_far[p, here, :] for p in range(pair_count)],
-                1,
-            )
-            field = tokens[here, :].astype(FULL) + contract(joined, weight_out[...], 1, 0)
-            resid[here, :] = field
-            unit, _ = layer_norm(field)
-            low_mid[place, :] = (unit * flat(gain_mid) + flat(shift_mid)).astype(LOW)
-
+        joined = jnp.concatenate(
+            [heads[p, own, :] for p in range(pair_count)]
+            + [heads_far[p] for p in range(pair_count)],
+            1,
+        )
+        field = tokens[...].astype(FULL) + contract(joined, weight_out[...], 1, 0)
+        resid[...] = field
+        unit, _ = layer_norm(field)
+        low_mid[own, :] = (unit * flat(gain_mid) + flat(shift_mid)).astype(LOW)
+        for i in range(2):
             mid_far(i).start()
-
 
         for one in up_loads:
             one.wait()
@@ -1092,7 +1088,9 @@
             def _():
                 fades[tile_rows(i - 2), pl.ds(0, width)] = part
 
-            steps_when(i == 1, "out gather", "early turn", "attn1 gather")
+            steps_when(i == 0, "out gather")
+            steps_when(i == 1, "early turn")
+            steps_when(i == 2, "attn1 gather")
             steps_when(i == 3, "lead turn")
 
         for i in range(2):

time: 103 us -> 102 us (level)
  no operation moved by 1% of the time
where the time goes in v5:
time: 102 us
  Pallas kernels  101 us (99%)
    pallas_call x1, Pallas kernels, layer(): pl.pallas_call(functools.partial(layer_kernel, fused), out_shape=outs, in...  98.1 us
    pallas_call x1, Pallas kernels, deliver(): pl.pallas_call(functools.partial(deliver_kernel, len(arrays)), out_shape=...  3.07 us

profile of v5, /device:TPU:1, one launch (start us, length us, event | category | flops | bytes accessed | tf_op | source)
XLA Modules:
  0.0 102.0 jit_solution(5359571539762947333)
XLA Ops:
  0.6 98.1 %layer.1 = (bf16[512,768]{1,0:T(8,128)(2,1)}, bf16[512,768]{1,0:T(8,128)(2,1)}, bf16[1,2,192,384]{3,2,1,0:T(8,128)(2,1)}, bf16[2,2,48,768]{3,2,1,0:T(8,128)(2,1)...) custom-call(bf16[512,768]{1,0:T(8,128)(2,1)} %bitcast.4, ...), custom_call_target="tpu_custom_call" | custom-call | tf_op jit(solution)/shard_map/layer/pallas_call | solution.py:1275
  98.8 3.1 %deliver.1 = (bf16[512,768]{1,0:T(8,128)(2,1)}, bf16[512,768]{1,0:T(8,128)(2,1)}, f32[1,512]{1,0:T(1,128)}, f32[48,768]{1,0:T(8,128)}, f32[48,768]{1,0:T(8,128)}...) custom-call(bf16[512,768]{1,0:T(8,128)(2,1)} %get-tuple-element.36.r, ...), custom_call_target="tpu_custom_call" | custom-call | tf_op jit(solution)/shard_map/deliver/pallas_call | solution.py:1349
